TPU v7x, 32 devices: a whole 2x2x4 slice. The times are simulated.
32 devices in a mesh: dp: 8 (over z, x), tensor: 4 (over y, core).
Axes of the slice: x: 2, y: 2, z: 4, core: 2. Of those that a mesh axis runs over, the one named last changes fastest.
Arguments:
- tokens: bfloat16 [8192, 1024], P(('dp', 'tensor')), may hold values from -6 to 6
- attn_gain: float32 [1024], replicated, may hold values from 0.5 to 1.5
- qkv_weight: bfloat16 [1024, 16, 192], P('dp', 'tensor'), may hold values from -0.1875 to 0.1875
- out_weight: bfloat16 [1024, 1024], P('tensor', 'dp'), may hold values from -4 to 4
- mlp_gain: float32 [1024], replicated, may hold values from 0.5 to 1.5
- in_weight: bfloat16 [1024, 2, 2624], P('dp', None, 'tensor'), may hold values from -0.1875 to 0.1875
- down_weight: bfloat16 [2624, 1024], P('tensor', 'dp'), may hold values from -0.125 to 0.125
- seg_lengths: int32 [8, 3], P('dp'), may hold values from 1 to 512, 1024 in all within a row
- cotangent: bfloat16 [8192, 1024], P(('dp', 'tensor')), may hold values from -12 to 12
Outputs:
- layer_out: bfloat16 [8192, 1024], P(('dp', 'tensor'))
- grad_tokens: bfloat16 [8192, 1024], P(('dp', 'tensor'))
- grad_attn_gain: float32 [1024], replicated
- grad_qkv_weight: float32 [1024, 16, 192], P('dp', 'tensor')
- grad_out_weight: float32 [1024, 1024], P('tensor', 'dp')
- grad_mlp_gain: float32 [1024], replicated
- grad_in_weight: float32 [1024, 2, 2624], P('dp', None, 'tensor')
- grad_down_weight: float32 [2624, 1024], P('tensor', 'dp')
Inputs may be any that keep to these rules, and one draw needn't show every extreme that they name: `seg_lengths`: row p holds the lengths of the 3 segments that fill pack p in order; they sum to 1024 and the longest is 512.
All inputs are finite; a program needn't handle non-finite values.
Results may differ from a plain program's by a relative error of at most 0.024.
Values may be sent and summed in bfloat16 or wider, within the bound.
A program may use at most 128 MiB of HBM per device.

v0:
```python
import math

import jax
import jax.numpy as jnp
from jax import lax
from jax.sharding import PartitionSpec as P

NORM_EPS = 1e-05
ROPE_BASE = 160000.0
HALF_ROOT = 0.7071067811865476
INV_ROOT_TAU = 0.3989422804014327
MASKED_SCORE = -1e30


def dot_plain(left, right):
    return jnp.dot(left, right, preferred_element_type=jnp.float32)


def dot_first(left, right):
    return lax.dot_general(
        left, right, (((0,), (0,)), ((), ())), preferred_element_type=jnp.float32
    )


def dot_last(left, right):
    return lax.dot_general(
        left, right, (((1,), (1,)), ((), ())), preferred_element_type=jnp.float32
    )


def layer_norm(row_data, norm_gain):
    centered = row_data - jnp.mean(row_data, axis=-1, keepdims=True)
    inverse = lax.rsqrt(jnp.mean(centered * centered, axis=-1, keepdims=True) + NORM_EPS)
    unit_rows = centered * inverse
    return (unit_rows * norm_gain, unit_rows, inverse)


def norm_back(grad_normed, unit_rows, inverse, norm_gain):
    scaled = grad_normed * norm_gain
    grad_rows = inverse * (
        scaled
        - jnp.mean(scaled, axis=-1, keepdims=True)
        - unit_rows * jnp.mean(scaled * unit_rows, axis=-1, keepdims=True)
    )
    return (grad_rows, jnp.sum(grad_normed * unit_rows, axis=0))


def gelu_parts(value_in):
    normal_cdf = 0.5 * (1.0 + lax.erf(value_in * HALF_ROOT))
    slope = normal_cdf + value_in * INV_ROOT_TAU * jnp.exp(-0.5 * value_in * value_in)
    return (value_in * normal_cdf, slope)


def segment_info(seg_lens, pack_rows):
    seg_ends = jnp.cumsum(seg_lens)
    places = lax.iota(jnp.int32, pack_rows)
    before = seg_ends[None, :] <= places[:, None]
    seg_ids = jnp.sum(before.astype(jnp.int32), axis=1)
    seg_first = jnp.sum(jnp.where(before, seg_lens[None, :], 0), axis=1)
    return (seg_ids, places - seg_first)


def rotary(position, head_dim):
    half_dim = head_dim // 2
    inv_freq = jnp.exp(lax.iota(jnp.float32, half_dim) * (-2.0 * math.log(ROPE_BASE) / head_dim))
    angles = position.astype(jnp.float32)[:, None] * inv_freq[None, :]
    return (jnp.cos(angles), jnp.sin(angles))


def turn(vectors, cos_table, sin_table):
    half_dim = vectors.shape[-1] // 2
    front_half = vectors[..., :half_dim]
    back_half = vectors[..., half_dim:]
    cos_part = cos_table[:, None, :]
    sin_part = sin_table[:, None, :]
    return jnp.concatenate(
        [
            front_half * cos_part - back_half * sin_part,
            back_half * cos_part + front_half * sin_part,
        ],
        axis=-1,
    )


def turn_back(grads_in, cos_table, sin_table):
    half_dim = grads_in.shape[-1] // 2
    front_half = grads_in[..., :half_dim]
    back_half = grads_in[..., half_dim:]
    cos_part = cos_table[:, None, :]
    sin_part = sin_table[:, None, :]
    return jnp.concatenate(
        [
            front_half * cos_part + back_half * sin_part,
            back_half * cos_part - front_half * sin_part,
        ],
        axis=-1,
    )


def block_scores(query_part, key_part, seg_query, seg_key, score_scale):
    scores = (
        jnp.einsum("qhd,khd->hqk", query_part, key_part, preferred_element_type=jnp.float32)
        * score_scale
    )
    return jnp.where((seg_query[:, None] == seg_key[None, :])[None], scores, MASKED_SCORE)


def attention_forward(query_rows, key_rows, value_rows, seg_ids, query_block, score_scale):
    pack_rows, heads_local, head_dim = query_rows.shape
    block_count = pack_rows // query_block

    def one_block(block_index):
        query_start = block_index * query_block
        query_part = lax.dynamic_slice_in_dim(query_rows, query_start, query_block, 0)
        seg_query = lax.dynamic_slice_in_dim(seg_ids, query_start, query_block, 0)
        scores = block_scores(query_part, key_rows, seg_query, seg_ids, score_scale)
        row_top = jnp.max(scores, axis=-1, keepdims=True)
        expo = jnp.exp(scores - row_top)
        row_total = jnp.sum(expo, axis=-1, keepdims=True)
        weights = (expo / row_total).astype(jnp.bfloat16)
        result = jnp.einsum("hqk,khd->qhd", weights, value_rows, preferred_element_type=jnp.float32)
        return (result, (row_top + jnp.log(row_total))[..., 0])

    results, log_totals = lax.map(one_block, jnp.arange(block_count, dtype=jnp.int32))
    return (results.reshape(pack_rows, heads_local, head_dim), log_totals)


def attention_backward(
    query_rows, key_rows, value_rows, grad_attended, log_totals, seg_ids, query_block, score_scale
):
    pack_rows, heads_local, head_dim = query_rows.shape
    block_count = pack_rows // query_block

    def block_step(running, block_index):
        grad_keys, grad_values = running
        query_start = block_index * query_block
        query_part = lax.dynamic_slice_in_dim(query_rows, query_start, query_block, 0)
        grad_part = lax.dynamic_slice_in_dim(grad_attended, query_start, query_block, 0)
        seg_query = lax.dynamic_slice_in_dim(seg_ids, query_start, query_block, 0)
        scores = block_scores(query_part, key_rows, seg_query, seg_ids, score_scale)
        probs = jnp.exp(scores - log_totals[block_index][..., None])
        grad_probs = jnp.einsum(
            "qhd,khd->hqk", grad_part, value_rows, preferred_element_type=jnp.float32
        )
        inner = jnp.sum(probs * grad_probs, axis=-1, keepdims=True)
        grad_scores = (probs * (grad_probs - inner)).astype(jnp.bfloat16) * score_scale
        grad_query_part = jnp.einsum(
            "hqk,khd->qhd", grad_scores, key_rows, preferred_element_type=jnp.float32
        )
        grad_key_part = jnp.einsum(
            "hqk,qhd->khd", grad_scores, query_part, preferred_element_type=jnp.float32
        )
        grad_value_part = jnp.einsum(
            "hqk,qhd->khd",
            probs.astype(jnp.bfloat16),
            grad_part,
            preferred_element_type=jnp.float32,
        )
        grad_keys = grad_keys + grad_key_part
        grad_values = grad_values + grad_value_part
        return ((grad_keys, grad_values), grad_query_part)

    empty_grad = jnp.zeros(query_rows.shape, jnp.float32)
    (grad_keys, grad_values), grad_queries = lax.scan(
        block_step, (empty_grad, empty_grad), jnp.arange(block_count, dtype=jnp.int32)
    )
    return (grad_queries.reshape(pack_rows, heads_local, head_dim), grad_keys, grad_values)


def body(
    tokens,
    attn_gain,
    qkv_weight,
    out_weight,
    mlp_gain,
    in_weight,
    down_weight,
    seg_lengths,
    cotangent,
):
    tok_dev, model_width = tokens.shape
    pack_rows = tok_dev * lax.axis_size("tensor")
    heads_local = qkv_weight.shape[1]
    head_dim = qkv_weight.shape[2] // 3
    hidden_local = in_weight.shape[2]
    score_scale = head_dim ** (-0.5)
    query_block = min(512, pack_rows)
    qkv_full, out_full, in_full, down_full = (
        lax.all_gather(qkv_weight, "dp", axis=0, tiled=True),
        lax.all_gather(out_weight, "dp", axis=1, tiled=True),
        lax.all_gather(in_weight, "dp", axis=0, tiled=True),
        lax.all_gather(down_weight, "dp", axis=1, tiled=True),
    )
    qkv_flat = qkv_full.reshape(model_width, heads_local * 3 * head_dim)
    seg_ids, position = segment_info(seg_lengths[0], pack_rows)
    cos_table, sin_table = rotary(position, head_dim)
    row_data = tokens.astype(jnp.float32)
    normed_attn, unit_attn, inverse_attn = layer_norm(row_data, attn_gain)
    attn_input = lax.all_gather(normed_attn.astype(jnp.bfloat16), "tensor", axis=0, tiled=True)
    mixed_proj = dot_plain(attn_input, qkv_flat).reshape(pack_rows, heads_local, 3, head_dim)
    query_rows = turn(mixed_proj[:, :, 0], cos_table, sin_table).astype(jnp.bfloat16)
    key_rows = turn(mixed_proj[:, :, 1], cos_table, sin_table).astype(jnp.bfloat16)
    value_rows = mixed_proj[:, :, 2].astype(jnp.bfloat16)
    attended, log_totals = attention_forward(
        query_rows, key_rows, value_rows, seg_ids, query_block, score_scale
    )
    attended = attended.reshape(pack_rows, heads_local * head_dim).astype(jnp.bfloat16)
    residual = row_data + lax.psum_scatter(
        dot_plain(attended, out_full).astype(jnp.bfloat16),
        "tensor",
        scatter_dimension=0,
        tiled=True,
    ).astype(jnp.float32)
    normed_mlp, unit_mlp, inverse_mlp = layer_norm(residual, mlp_gain)
    mlp_input = normed_mlp.astype(jnp.bfloat16)
    mlp_rows = lax.all_gather(mlp_input, "tensor", axis=0, tiled=True)
    in_flat = in_full.reshape(model_width, -1)
    lifted = dot_plain(mlp_rows, in_flat).reshape(pack_rows, 2, hidden_local)
    act_gelu, act_slope = gelu_parts(lifted[:, 0])
    activated = (act_gelu * lifted[:, 1]).astype(jnp.bfloat16)
    layer_out = (
        residual
        + lax.psum_scatter(
            dot_plain(activated, down_full).astype(jnp.bfloat16),
            "tensor",
            scatter_dimension=0,
            tiled=True,
        ).astype(jnp.float32)
    ).astype(jnp.bfloat16)
    cotangent_rows = lax.all_gather(cotangent, "tensor", axis=0, tiled=True)
    grad_act = dot_last(cotangent_rows, down_full)
    grad_lifted = jnp.concatenate(
        [grad_act * lifted[:, 1] * act_slope, grad_act * act_gelu], axis=1
    ).astype(jnp.bfloat16)
    grad_mlp_in = lax.psum_scatter(
        dot_last(grad_lifted, in_flat).astype(jnp.bfloat16),
        "tensor",
        scatter_dimension=0,
        tiled=True,
    ).astype(jnp.float32)
    grad_in_part = dot_first(mlp_rows, grad_lifted).reshape(in_full.shape)
    grad_down_part = dot_first(activated, cotangent_rows)
    grad_resid_norm, mlp_gain_part = norm_back(grad_mlp_in, unit_mlp, inverse_mlp, mlp_gain)
    grad_residual = cotangent.astype(jnp.float32) + grad_resid_norm
    grad_branch = lax.all_gather(grad_residual.astype(jnp.bfloat16), "tensor", axis=0, tiled=True)
    grad_out_part = dot_first(attended, grad_branch)
    grad_attended = (
        dot_last(grad_branch, out_full)
        .astype(jnp.bfloat16)
        .reshape(pack_rows, heads_local, head_dim)
    )
    grad_queries, grad_keys, grad_values = attention_backward(
        query_rows,
        key_rows,
        value_rows,
        grad_attended,
        log_totals,
        seg_ids,
        query_block,
        score_scale,
    )
    grad_mixed = jnp.stack(
        [
            turn_back(grad_queries, cos_table, sin_table),
            turn_back(grad_keys, cos_table, sin_table),
            grad_values,
        ],
        axis=2,
    )
    grad_mixed = grad_mixed.reshape(pack_rows, heads_local * 3 * head_dim).astype(jnp.bfloat16)
    grad_qkv_part = dot_first(attn_input, grad_mixed).reshape(qkv_full.shape)
    grad_attn_in = lax.psum_scatter(
        dot_last(grad_mixed, qkv_flat).astype(jnp.bfloat16),
        "tensor",
        scatter_dimension=0,
        tiled=True,
    ).astype(jnp.float32)
    grad_rows_attn, attn_gain_part = norm_back(grad_attn_in, unit_attn, inverse_attn, attn_gain)
    grad_tokens = (grad_residual + grad_rows_attn).astype(jnp.bfloat16)
    qkv_grad, out_grad, in_grad, down_grad = (
        lax.psum_scatter(
            grad_qkv_part.astype(jnp.bfloat16), "dp", scatter_dimension=0, tiled=True
        ).astype(jnp.float32),
        lax.psum_scatter(
            grad_out_part.astype(jnp.bfloat16), "dp", scatter_dimension=1, tiled=True
        ).astype(jnp.float32),
        lax.psum_scatter(
            grad_in_part.astype(jnp.bfloat16), "dp", scatter_dimension=0, tiled=True
        ).astype(jnp.float32),
        lax.psum_scatter(
            grad_down_part.astype(jnp.bfloat16), "dp", scatter_dimension=1, tiled=True
        ).astype(jnp.float32),
    )
    attn_gain_grad, mlp_gain_grad = lax.psum((attn_gain_part, mlp_gain_part), ("dp", "tensor"))
    return (
        layer_out,
        grad_tokens,
        attn_gain_grad,
        qkv_grad,
        out_grad,
        mlp_gain_grad,
        in_grad,
        down_grad,
    )


def solution(mesh):
    in_specs = (
        P(("dp", "tensor"), None),
        P(),
        P("dp", "tensor", None),
        P("tensor", "dp"),
        P(),
        P("dp", None, "tensor"),
        P("tensor", "dp"),
        P("dp", None),
        P(("dp", "tensor"), None),
    )
    out_specs = (
        P(("dp", "tensor"), None),
        P(("dp", "tensor"), None),
        P(),
        P("dp", "tensor", None),
        P("tensor", "dp"),
        P(),
        P("dp", None, "tensor"),
        P("tensor", "dp"),
    )
    return jax.shard_map(body, mesh=mesh, in_specs=in_specs, out_specs=out_specs, check_vma=False)
```

profile of v0, /device:TPU:0, one launch (start us, length us, event | category | flops | bytes accessed | tf_op | source)
XLA Modules:
  0.0 726.5 jit_solution(4247788537337748045)
XLA Ops:
  9.2 1.3 fusion.112
  11.1 2.1 fusion.107
  13.6 30.7 %all_gather.26 = bf16[256,1024]{1,0:T(8,128)(2,1)S(1)} all-gather(bf16[256,128]{1,0:T(8,128)(2,1)S(1)} %copy-done.18), channel_id=1, replica_groups=mesh['dp'=8,'tensor'=4] {'dp'}, dimensions={1}, use_global_device_ids=true | all-gather | bytes 589824 | tf_op jit(solution)/shard_map/all_gather | solution.py:190
  44.9 16.9 %all-gather.10.cloned.1.call-done = bf16[1024,4,192]{0,2,1:T(8,128)(2,1)} async-done(((bf16[128,4,192]{0,2,1:T(8,128)(2,1)}), bf16[1024,4,192]{0,2,1:T(8,128)(2,1)}) %all-gather.10.cloned.1.call-update) | async-done | bytes 1572880 | tf_op jit(solution)/shard_map/all_gather | solution.py:189
  61.8 23.0 %all-gather.8.cloned.1.call-done = bf16[1024,1024]{1,0:T(8,128)(2,1)} async-done(((bf16[256,1024]{1,0:T(8,128)(2,1)}), bf16[1024,1024]{1,0:T(8,128)(2,1)}) %all-gather.8.cloned.1.call-update) | async-done | bytes 2097168 | tf_op jit(solution)/shard_map/all_gather | solution.py:199
  84.8 3.9 fusion.89
  89.4 19.1 %while.27 = (s32[]{:T(128)}, bf16[2,512,4,64]{1,3,2,0:T(8,128)(2,1)}, f32[2,4,512]{2,1,0:T(4,128)S(1)}, s32[2]{0:T(128)S(1)}, s32[1024]{0:T(1024)S(1)}, /*index=...) while((s32[]{:T(128)}, ...), condition=%wide.region_8.9_spmd, body=%wide.region_5.8_spmd.sunk | while | flops 562558976 | bytes 33368320 | solution.py:124
  91.1 1.7 fusion.172
  92.8 2.3 fusion.173
  95.2 3.0 fusion.174
  100.7 1.7 fusion.172
  102.4 2.3 fusion.173
  104.7 3.0 fusion.174
  108.6 1.6 copy.28
  111.0 2.1 convolution_convert_fusion.2
  113.7 30.9 %reduce-scatter.17.cloned.1.call-done = bf16[256,1024]{1,0:T(8,128)(2,1)} async-done(((bf16[1024,1024]{1,0:T(8,128)(2,1)}), bf16[256,1024]{1,0:T(8,128)(2,1)}) %reduce-scatter.17.cloned.1.call-update) | async-done | bytes 524304 | tf_op jit(solution)/shard_map/reduce_scatter | solution.py:208
  146.0 1.3 multiply_reduce_fusion.1
  147.3 2.1 multiply_convert_fusion.3
  151.0 53.5 %all-gather.14.cloned.1.call-done = bf16[1024,2,656]{0,2,1:T(8,128)(2,1)} async-done(((bf16[128,2,656]{0,2,1:T(8,128)(2,1)}), bf16[1024,2,656]{0,2,1:T(8,128)(2,1)}) %all-gather.14.cloned.1.call-update) | async-done | bytes 2686992 | tf_op jit(solution)/shard_map/all_gather | solution.py:191
  204.5 22.9 %all-gather.12.cloned.1.call-done = bf16[1024,1024]{1,0:T(8,128)(2,1)} async-done(((bf16[256,1024]{1,0:T(8,128)(2,1)}), bf16[1024,1024]{1,0:T(8,128)(2,1)}) %all-gather.12.cloned.1.call-update) | async-done | bytes 2097168 | tf_op jit(solution)/shard_map/all_gather | solution.py:216
  227.3 7.7 %fusion.86 = f32[1024,2,656]{0,2,1:T(8,128)} fusion(bf16[1024,2,656]{0,2,1:T(8,128)(2,1)} %all-gather.14.cloned.1.call-done, bf16[1024,1024]{1,0:T(8,128)(2,1)} %all-gather.12.cloned.1.call-done), kind=kOutput, calls=%fused_computation.71 | convolution fusion | flops 2751463424 | bytes 10158080 | tf_op jit(solution)/shard_map/dot_general | solution.py:16
  235.1 37.0 %all-gather.16.cloned.1.call-done = bf16[656,1024]{1,0:T(8,128)(2,1)} async-done(((bf16[656,128]{1,0:T(8,128)(2,1)}), bf16[656,1024]{1,0:T(8,128)(2,1)}) %all-gather.16.cloned.1.call-update) | async-done | bytes 1343504 | tf_op jit(solution)/shard_map/all_gather | solution.py:192
  272.1 22.9 %all-gather.18.cloned.1.call-done = bf16[1024,1024]{1,0:T(8,128)(2,1)} async-done(((bf16[256,1024]{1,0:T(8,128)(2,1)}), bf16[1024,1024]{1,0:T(8,128)(2,1)}) %all-gather.18.cloned.1.call-update) | async-done | bytes 2097168 | tf_op jit(solution)/shard_map/all_gather | solution.py:230
  295.0 7.5 %fusion.85 = (bf16[1024,656]{0,1:T(8,128)(2,1)S(1)}, bf16[1024,656]{0,1:T(8,128)(2,1)S(1)}, bf16[1024,656]{0,1:T(8,128)(2,1)}) fusion(f32[1024,2,656]{0,2,1:T(8,128)} %fusion.86, bf16[1024,1024]{1,0:T(8,128)(2,1)} %all-gather.18.cloned.1.call-done, bf16[656,1024]{1,0:T(8,128)(2,1)} %all-gather.16.cloned.1.call-done), kind=kOutput, calls=%fused_computation.67 | convolution fusion | flops 1386479616 | bytes 12845056 | tf_op jit(solution)/shard_map/dot_general | solution.py:26
  304.0 4.6 convolution_convert_fusion.1
  308.7 31.5 %reduce-scatter.21.cloned.1.call-done = bf16[256,1024]{1,0:T(8,128)(2,1)} async-done(((bf16[1024,1024]{1,0:T(8,128)(2,1)}), bf16[256,1024]{1,0:T(8,128)(2,1)}) %reduce-scatter.21.cloned.1.call-update) | async-done | bytes 524304 | tf_op jit(solution)/shard_map/reduce_scatter | solution.py:235
  340.2 1.6 fusion.117
  341.9 2.4 fusion.124
  344.3 4.7 convolution_convert_fusion.5
  349.0 2.5 copy.38
  351.7 7.2 convolution_convert_fusion
  358.9 4.5 copy.42
  363.7 3.3 all-gather.20.cloned.1.call-done
  367.0 3.3 convolution_convert_fusion.6
  370.3 2.0 copy.34
  372.3 3.1 convolution_convert_fusion.7
  375.5 134.3 %while.28 = (s32[]{:T(128)}, f32[1024,4,64]{0,2,1:T(8,128)}, f32[1024,4,64]{0,2,1:T(8,128)}, f32[2,512,4,64]{1,0,3,2:T(2,128)}, s32[2]{0:T(128)S(1)}, /*index=5*...) while((s32[]{:T(128)}, f32[1024,4,64]{0,2,1:T(8,128)}, ...), condition=%wide.region_18.19_spmd.clone, body=%wide.region_16.18_spmd.clone.sunk | while | flops 1410865152 | bytes 123267416 | solution.py:164
  379.1 1.3 fusion.188
  380.4 3.6 fusion.190
  384.1 4.5 fusion.187
  388.6 18.1 %fusion.191 = f32[1,512,4,64]{1,3,2,0:T(8,128)} fusion(bf16[1024,4,64]{0,2,1:T(8,128)(2,1)S(1)} %get-tuple-element.419, f32[4,512,1024]{2,1,0:T(8,128)} %fusion.187, f32[4,512,1024]{2,1,0:T(8,128)} %copy-done, f32[4,512]{1,0:T(4,128)S(1)} %dynamic-slice_bitcast_fusion.2, pred[512,1024]{1,0:T(8,128)(4,1)S(1)} %broadcast_compare_fusion.5), kind=kOutput, calls=%fused_computation.37.clone.1 | convolution fusion | flops 297798656 | bytes 18358272 | tf_op jit(solution)/shard_map/while/body/eval_jaxpr/hqk,khd->qhd/dot_general | solution.py:147
  406.6 23.1 %fusion.189 = f32[1024,4,64]{0,2,1:T(8,128)} fusion(f32[4,512,1024]{2,1,0:T(8,128)} %fusion.187, f32[4,512,1024]{2,1,0:T(8,128)} %copy-done, f32[4,512]{1,0:T(4,128)S(1)} %dynamic-slice_bitcast_fusion.2, pred[512,1024]{1,0:T(8,128)(4,1)S(1)} %broadcast_compare_fusion.5, f32[1024,4,64]{0,2,1:T(8,128)} %get-tuple-element.397, pred[]{:T(512)S(6)} %compare.3, ...), kind=kOutput, calls=%fused_computation.35.clone.1 | convolution fusion | flops 298322944 | bytes 36978692 | tf_op jit(solution)/shard_map/while/body/eval_jaxpr/hqk,qhd->khd/dot_general | solution.py:150
  429.8 1.6 copy.59
  431.4 10.3 %dynamic_update_slice.19 = f32[2,512,4,64]{1,0,3,2:T(2,128)} dynamic-update-slice(f32[2,512,4,64]{1,0,3,2:T(2,128)} %get-tuple-element.399, f32[1,512,4,64]{1,0,3,2:T(1,128)S(1)} %copy.59, s32[]{:T(128)S(6)} %copy.76, s32[]{:T(128)} %constant.35.clone.1..sunk.1, s32[]{:T(128)} %constant.35.clone.1..sunk.1, s32[]{:T(128)} %constant.35.clone.1..sunk.1) | dynamic-update-slice | bytes 1048580 | tf_op jit(solution)/shard_map/while/body/jit(dynamic_update_index_in_dim)/dynamic_update_slice | solution.py:124
  445.3 1.3 fusion.188
  446.7 5.0 fusion.190
  451.7 4.5 fusion.187
  456.2 18.2 %fusion.191 = f32[1,512,4,64]{1,3,2,0:T(8,128)} fusion(bf16[1024,4,64]{0,2,1:T(8,128)(2,1)S(1)} %get-tuple-element.419, f32[4,512,1024]{2,1,0:T(8,128)} %fusion.187, f32[4,512,1024]{2,1,0:T(8,128)} %copy-done, f32[4,512]{1,0:T(4,128)S(1)} %dynamic-slice_bitcast_fusion.2, pred[512,1024]{1,0:T(8,128)(4,1)S(1)} %broadcast_compare_fusion.5), kind=kOutput, calls=%fused_computation.37.clone.1 | convolution fusion | flops 297798656 | bytes 18358272 | tf_op jit(solution)/shard_map/while/body/eval_jaxpr/hqk,khd->qhd/dot_general | solution.py:147
  474.4 23.2 %fusion.189 = f32[1024,4,64]{0,2,1:T(8,128)} fusion(f32[4,512,1024]{2,1,0:T(8,128)} %fusion.187, f32[4,512,1024]{2,1,0:T(8,128)} %copy-done, f32[4,512]{1,0:T(4,128)S(1)} %dynamic-slice_bitcast_fusion.2, pred[512,1024]{1,0:T(8,128)(4,1)S(1)} %broadcast_compare_fusion.5, f32[1024,4,64]{0,2,1:T(8,128)} %get-tuple-element.397, pred[]{:T(512)S(6)} %compare.3, ...), kind=kOutput, calls=%fused_computation.35.clone.1 | convolution fusion | flops 298322944 | bytes 36978692 | tf_op jit(solution)/shard_map/while/body/eval_jaxpr/hqk,qhd->khd/dot_general | solution.py:150
  497.6 1.6 copy.59
  499.2 10.3 %dynamic_update_slice.19 = f32[2,512,4,64]{1,0,3,2:T(2,128)} dynamic-update-slice(f32[2,512,4,64]{1,0,3,2:T(2,128)} %get-tuple-element.399, f32[1,512,4,64]{1,0,3,2:T(1,128)S(1)} %copy.59, s32[]{:T(128)S(6)} %copy.76, s32[]{:T(128)} %constant.35.clone.1..sunk.1, s32[]{:T(128)} %constant.35.clone.1..sunk.1, s32[]{:T(128)} %constant.35.clone.1..sunk.1) | dynamic-update-slice | bytes 1048580 | tf_op jit(solution)/shard_map/while/body/jit(dynamic_update_index_in_dim)/dynamic_update_slice | solution.py:124
  509.8 2.2 reshape.258
  512.1 1.5 multiply_add_fusion.1
  513.7 1.6 maximum_convert_fusion
  515.6 3.0 fusion.94
  518.6 2.7 copy.40
  521.3 4.6 convolution_convert_fusion.3
  526.0 4.9 convolution_convert_fusion.4
  535.0 40.3 %reduce-scatter.27.cloned.1.call-done = bf16[128,256]{1,0:T(8,128)(2,1)} async-done(((bf16[1024,256]{1,0:T(8,128)(2,1)}), bf16[128,256]{1,0:T(8,128)(2,1)}) %reduce-scatter.27.cloned.1.call-update) | async-done | bytes 65552
  577.0 65.6 %reduce-scatter.25.cloned.1.call-done = bf16[128,768]{1,0:T(8,128)(2,1)} async-done(((bf16[1024,768]{1,0:T(8,128)(2,1)}), bf16[128,768]{1,0:T(8,128)(2,1)}) %reduce-scatter.25.cloned.1.call-update) | async-done | bytes 196624
  644.4 31.0 %reduce-scatter.23.cloned.1.call-done = bf16[256,1024]{1,0:T(8,128)(2,1)} async-done(((bf16[1024,1024]{1,0:T(8,128)(2,1)}), bf16[256,1024]{1,0:T(8,128)(2,1)}) %reduce-scatter.23.cloned.1.call-update) | async-done | bytes 524304 | tf_op jit(solution)/shard_map/reduce_scatter | solution.py:272
  675.5 1.6 fusion.119
  677.1 39.5 %all-reduce = (f32[1024]{0:T(1024)}, f32[1024]{0:T(1024)}) all-reduce(f32[1024]{0:T(1024)S(1)} %get-tuple-element.153, f32[1024]{0:T(1024)S(1)} %get-tuple-element.151), channel_id=1, replica_groups=mesh['dp'=8,'tensor'=4] {'dp','tensor'}, use_global_device_ids=true, to_apply=%region_23.24 | all-reduce | flops 2048 | bytes 16384 | tf_op jit(solution)/shard_map/psum | solution.py:294
  716.6 3.0 fusion.111
  (155 shorter events, 24.3 us)
Async XLA Ops:
  7.2 6.2 copy-start.25
  7.2 6.5 copy-start.18
  7.2 54.6 %all-gather.10.cloned.1.call-start = ((), (), s32[]{:S(2)}) async-start(), calls=%async_computation.9 | async-start | bytes 1769472 | tf_op jit(solution)/shard_map/all_gather | solution.py:189
  7.9 76.8 %all-gather.8.cloned.1.call-start = ((), (), s32[]{:S(2)}) async-start(), calls=%async_computation.8 | async-start | bytes 2621440 | tf_op jit(solution)/shard_map/all_gather | solution.py:199
  9.2 1.4 copy-start.21
  10.5 0.6 copy-start.23
  13.2 131.5 %reduce-scatter.17.cloned.1.call-start = ((), (), s32[]{:S(2)}) async-start(), calls=%async_computation.10 | async-start | bytes 2621440 | tf_op jit(solution)/shard_map/reduce_scatter | solution.py:208
  44.4 65.9 %copy-start.7 = (bf16[256,1024]{1,0:T(8,128)(2,1)}, bf16[256,1024]{1,0:T(8,128)(2,1)S(1)}, u32[]{:S(2)}) copy-start(bf16[256,1024]{1,0:T(8,128)(2,1)S(1)} %all_gather.26) | copy-start | bytes 1572868
  44.9 44.1 %copy-start.12 = (f32[1024,32]{0,1:T(8,128)}, f32[1024,32]{0,1:T(8,128)S(1)}, u32[]{:S(2)}) copy-start(f32[1024,32]{0,1:T(8,128)S(1)} %get-tuple-element.220) | copy-start | bytes 393220
  44.9 44.1 %copy-start.14 = (f32[1024,32]{0,1:T(8,128)}, f32[1024,32]{0,1:T(8,128)S(1)}, u32[]{:S(2)}) copy-start(f32[1024,32]{0,1:T(8,128)S(1)} %get-tuple-element.221) | copy-start | bytes 393220
  92.8 2.3 copy-start.16
  98.2 0.8 copy-start.17
  102.4 2.3 copy-start.16
  107.8 0.8 copy-start.17
  110.2 0.8 copy-start.9
  111.0 33.7 %copy-start.1 = (bf16[256,1024]{1,0:T(8,128)(2,1)S(1)}, bf16[256,1024]{1,0:T(8,128)(2,1)}, u32[]{:S(2)}) copy-start(bf16[256,1024]{1,0:T(8,128)(2,1)} %param.13) | copy-start | bytes 1572868
  113.1 34.2 %copy-start.19 = (f32[1024]{0:T(1024)S(1)}, f32[1024]{0:T(1024)}, u32[]{:S(2)}) copy-start(f32[1024]{0:T(1024)} %param.17) | copy-start | bytes 12292
  113.1 91.4 %all-gather.14.cloned.1.call-start = ((), (), s32[]{:S(2)}) async-start(), calls=%async_computation.12 | async-start | bytes 3022848 | tf_op jit(solution)/shard_map/all_gather | solution.py:191
  113.7 113.6 %all-gather.12.cloned.1.call-start = ((), (), s32[]{:S(2)}) async-start(), calls=%async_computation.11 | async-start | bytes 2621440 | tf_op jit(solution)/shard_map/all_gather | solution.py:216
  149.4 122.7 %all-gather.16.cloned.1.call-start = ((), (), s32[]{:S(2)}) async-start(), calls=%async_computation.13 | async-start | bytes 1511424 | tf_op jit(solution)/shard_map/all_gather | solution.py:192
  150.0 145.0 %all-gather.18.cloned.1.call-start = ((), (), s32[]{:S(2)}) async-start(), calls=%async_computation.15 | async-start | bytes 2621440 | tf_op jit(solution)/shard_map/all_gather | solution.py:230
  150.8 189.5 %reduce-scatter.21.cloned.1.call-start = ((), (), s32[]{:S(2)}) async-start(), calls=%async_computation.16 | async-start | bytes 2621440 | tf_op jit(solution)/shard_map/reduce_scatter | solution.py:235
  295.0 9.0 %copy-start.26 = (bf16[1024,2,656]{0,2,1:T(8,128)(2,1)S(1)}, bf16[1024,2,656]{0,2,1:T(8,128)(2,1)}, u32[]{:S(2)}) copy-start(bf16[1024,2,656]{0,2,1:T(8,128)(2,1)} %all-gather.14.cloned.1.call-done) | copy-start | bytes 8060932
  302.5 1.1 copy-start.28
  302.5 1.5 copy-start.29
  304.0 36.3 %copy-start.2 = (bf16[256,1024]{1,0:T(8,128)(2,1)S(1)}, bf16[256,1024]{1,0:T(8,128)(2,1)}, u32[]{:S(2)}) copy-start(bf16[256,1024]{1,0:T(8,128)(2,1)} %reduce-scatter.17.cloned.1.call-done) | copy-start | bytes 1572868
  308.6 33.3 %copy-start.4 = (bf16[256,1024]{1,0:T(8,128)(2,1)S(1)}, bf16[256,1024]{1,0:T(8,128)(2,1)}, u32[]{:S(2)}) copy-start(bf16[256,1024]{1,0:T(8,128)(2,1)} %param.21) | copy-start | bytes 1572868
  308.6 58.4 %all-gather.20.cloned.1.call-start = ((), (), s32[]{:S(2)}) async-start(), calls=%async_computation.17 | async-start | bytes 2621440 | tf_op jit(solution)/shard_map/all_gather | solution.py:245
  344.3 186.7 %reduce-scatter.31.cloned.1.call-start = ((), (), s32[]{:S(2)}) async-start(), calls=%async_computation.22 | async-start | bytes 1769472
  351.6 181.3 %reduce-scatter.29.cloned.1.call-start = ((), (), s32[]{:S(2)}) async-start(), calls=%async_computation.21 | async-start | bytes 3244032
  363.4 8.9 %copy-start.8 = (bf16[256,1024]{1,0:T(8,128)(2,1)S(1)}, bf16[256,1024]{1,0:T(8,128)(2,1)}, u32[]{:S(2)}) copy-start(bf16[256,1024]{1,0:T(8,128)(2,1)} %copy-done.7) | copy-start | bytes 1572868
  363.4 211.9 %reduce-scatter.27.cloned.1.call-start = ((), (), s32[]{:S(2)}) async-start(), calls=%async_computation.20 | async-start | bytes 589824
  379.1 1.3 copy-start.6
  380.4 3.6 copy-start
  445.3 1.3 copy-start.6
  446.7 5.0 copy-start
  509.8 2.3 copy-start.13
  509.8 2.3 copy-start.15
  512.0 130.6 %reduce-scatter.25.cloned.1.call-start = ((), (), s32[]{:S(2)}) async-start(), calls=%async_computation.19 | async-start | bytes 1769472
  513.7 1.9 copy-start.27
  515.4 3.2 copy-start.10
  518.6 2.8 copy-start.11
  521.3 154.2 %reduce-scatter.23.cloned.1.call-start = ((), (), s32[]{:S(2)}) async-start(), calls=%async_computation.18 | async-start | bytes 2621440 | tf_op jit(solution)/shard_map/reduce_scatter | solution.py:272
  525.9 190.6 %reduce-scatter.19.cloned.1.call-start = ((), (), s32[]{:S(2)}) async-start(), calls=%async_computation.14 | async-start | bytes 2621440 | tf_op jit(solution)/shard_map/reduce_scatter | solution.py:223
  530.9 144.6 %copy-start.20 = (f32[1024]{0:T(1024)S(1)}, f32[1024]{0:T(1024)}, u32[]{:S(2)}) copy-start(f32[1024]{0:T(1024)} %param.14) | copy-start | bytes 12292
  530.9 144.6 %copy-start.22 = (f32[256]{0:T(256)S(1)}, f32[256]{0:T(256)}, u32[]{:S(2)}) copy-start(f32[256]{0:T(256)} %copy-done.21) | copy-start | bytes 3076
  530.9 144.6 %copy-start.24 = (f32[256]{0:T(256)S(1)}, f32[256]{0:T(256)}, u32[]{:S(2)}) copy-start(f32[256]{0:T(256)} %copy-done.23) | copy-start | bytes 3076
  530.9 185.6 %copy-start.3 = (bf16[256,1024]{1,0:T(8,128)(2,1)S(1)}, bf16[256,1024]{1,0:T(8,128)(2,1)}, u32[]{:S(2)}) copy-start(bf16[256,1024]{1,0:T(8,128)(2,1)} %reduce-scatter.21.cloned.1.call-done) | copy-start | bytes 1572868
  530.9 185.6 %copy-start.5 = (bf16[256,1024]{1,0:T(8,128)(2,1)S(1)}, bf16[256,1024]{1,0:T(8,128)(2,1)}, u32[]{:S(2)}) copy-start(bf16[256,1024]{1,0:T(8,128)(2,1)} %param.21) | copy-start | bytes 1572868
Sparse Core Ops, SparseCore 0:
  10.1 51.6 all-gather.9
  63.9 20.7 all-gather.7
  113.2 31.4 reduce-scatter.16
  146.8 57.6 all-gather.13
  206.5 20.7 all-gather.11
  229.4 42.5 all-gather.15
  273.7 21.2 all-gather.17
  308.8 31.4 reduce-scatter.20
  344.4 22.5 all-gather.19
  370.3 65.0 reduce-scatter.30
  439.4 70.6 reduce-scatter.28
  514.2 61.0 reduce-scatter.26
  578.8 63.7 reduce-scatter.24
  645.1 30.3 reduce-scatter.22
  677.8 31.5 reduce-scatter.18
where the time goes:
time: 736 us; the launch traced here: 727 us
  waiting for transfers between devices  382 us (52%)
  matrix products  169 us (23%)
  blocking collectives  70.2 us (10%)
  local copies, waits for them, and re-layouts  51.6 us (7%)
  other arithmetic  31.6 us (4%)
  between operations  14.8 us (2%)
    unnamed x19, waiting for transfers between devices  109 us
    all_gather x1, waiting for transfers between devices, body(): lax.all_gather(in_weight, 'dp', axis=0, tiled=True)  53.5 us
    dot_general x2, matrix products, block_step(): jnp.einsum('hqk,qhd->khd', grad_scores, query_part, preferred_element_typ...  46.3 us
    psum x1, blocking collectives, body(): lax.psum((attn_gain_part, mlp_gain_part), ('dp', 'tensor'))  39.5 us
    all_gather x1, waiting for transfers between devices, body(): lax.all_gather(down_weight, 'dp', axis=1, tiled=True)  37 us
    dot_general x2, matrix products, block_step(): jnp.einsum('hqk,khd->qhd', grad_scores, key_rows, preferred_element_type=...  36.3 us
    reduce_scatter x1, waiting for transfers between devices, body(): lax.psum_scatter(dot_last(grad_lifted, in_flat).astype(jnp.bfloat16), 'te...  31.5 us
    reduce_scatter x1, waiting for transfers between devices, body(): lax.psum_scatter(dot_last(grad_mixed, qkv_flat).astype(jnp.bfloat16), 'te...  31 us
  transfers between devices with their start and end apart: 15, of which 12 were waited for; matrix products, arithmetic and copies ran while one was open for 28% of the time, Pallas kernels for 0%

commit v1 on v0

--- a/solution.py
+++ b/solution.py
@@ -3,6 +3,8 @@
 import jax
 import jax.numpy as jnp
 from jax import lax
+from jax.experimental import pallas as pl
+from jax.experimental.pallas import tpu as pltpu
 from jax.sharding import PartitionSpec as P
 
 NORM_EPS = 1e-05
@@ -26,6 +28,520 @@
     return lax.dot_general(
         left, right, (((1,), (1,)), ((), ())), preferred_element_type=jnp.float32
     )
+
+
+MESH_ID = pl.DeviceIdType.MESH
+VM = pltpu.VMEM
+BF = jnp.bfloat16
+F32 = jnp.float32
+DMA = pltpu.SemaphoreType.DMA
+SPLIT = 4
+
+
+def swap_halves(wide):
+    width = wide.shape[1]
+    lane = lax.broadcasted_iota(jnp.int32, wide.shape, 1) % 64
+    return jnp.where(lane < 32, pltpu.roll(wide, width - 32, 1), pltpu.roll(wide, 32, 1))
+
+
+def attend_kernel(mixed_ref, cos_ref, sin_ref, segc_ref, segr_ref, qkv_ref, att_ref, lse_ref):
+    mixed = mixed_ref[...]
+    qkv_ref[...] = (mixed * cos_ref[...] + swap_halves(mixed) * sin_ref[...]).astype(BF)
+    rows = mixed_ref.shape[0]
+    block = 256
+    for head in range(2):
+        base = head * 192
+        keys = qkv_ref[:, base + 64 : base + 128]
+        values_t = qkv_ref[:, base + 128 : base + 192].astype(F32).T.astype(BF)
+
+        def step(i, carry):
+            start = pl.multiple_of(i * block, block)
+            query = qkv_ref[pl.ds(start, block), base : base + 64] * BF(0.125)
+            scores = dot_last(keys, query)
+            same = segc_ref[...] == segr_ref[:, pl.ds(start, block)]
+            scores = jnp.where(same, scores, MASKED_SCORE)
+            top = jnp.max(scores, axis=0, keepdims=True)
+            expo = jnp.exp(scores - top)
+            total = jnp.sum(expo, axis=0, keepdims=True)
+            weights = (expo * (1.0 / total)).astype(BF)
+            out_t = dot_plain(values_t, weights)
+            att_ref[pl.ds(start, block), head * 64 : head * 64 + 64] = out_t.T.astype(BF)
+            lse_ref[0, head : head + 1, pl.ds(start, block)] = top + jnp.log(total)
+            return carry
+
+        lax.fori_loop(0, rows // block, step, 0)
+
+
+def attend_back_kernel(qkv_ref, ga_ref, lse_ref, cos_ref, sin_ref, segc_ref, segr_ref, gm_ref, acc):
+    rows = qkv_ref.shape[0]
+    block = 256
+    for head in range(2):
+        base = head * 192
+        keys = qkv_ref[:, base + 64 : base + 128]
+        keys_t = keys.astype(F32).T.astype(BF)
+        values = qkv_ref[:, base + 128 : base + 192]
+
+        def step(i, carry):
+            grad_k, grad_v = carry
+            start = pl.multiple_of(i * block, block)
+            query = qkv_ref[pl.ds(start, block), base : base + 64] * BF(0.125)
+            grad_o = ga_ref[pl.ds(start, block), head * 64 : head * 64 + 64]
+            scores = dot_last(keys, query)
+            same = segc_ref[...] == segr_ref[:, pl.ds(start, block)]
+            scores = jnp.where(same, scores, MASKED_SCORE)
+            probs = jnp.exp(scores - lse_ref[0, head : head + 1, pl.ds(start, block)])
+            grad_p = dot_last(values, grad_o)
+            inner = jnp.sum(probs * grad_p, axis=0, keepdims=True)
+            grad_s = (probs * (grad_p - inner)).astype(BF)
+            grad_v = grad_v + dot_plain(probs.astype(BF), grad_o)
+            grad_k = grad_k + dot_plain(grad_s, query)
+            grad_q = dot_plain(keys_t, grad_s) * 0.125
+            acc[pl.ds(start, block), base : base + 64] = grad_q.T
+            return grad_k, grad_v
+
+        empty = jnp.zeros((rows, 64), F32)
+        grad_k, grad_v = lax.fori_loop(0, rows // block, step, (empty, empty))
+        acc[:, base + 64 : base + 128] = grad_k
+        acc[:, base + 128 : base + 192] = grad_v
+    grads = acc[...]
+    gm_ref[...] = (grads * cos_ref[...] - swap_halves(grads) * sin_ref[...]).astype(BF)
+
+
+def attend(mixed, cos_wide, sin_wide, seg_col, seg_row):
+    rows, cols = mixed.shape
+    pairs = cols // 384
+    whole = lambda p: (0, 0)
+    return pl.pallas_call(
+        attend_kernel,
+        grid=(pairs,),
+        in_specs=[
+            pl.BlockSpec((rows, 384), lambda p: (0, p)),
+            pl.BlockSpec((rows, 384), whole),
+            pl.BlockSpec((rows, 384), whole),
+            pl.BlockSpec((rows, 1), whole),
+            pl.BlockSpec((1, rows), whole),
+        ],
+        out_specs=[
+            pl.BlockSpec((rows, 384), lambda p: (0, p)),
+            pl.BlockSpec((rows, 128), lambda p: (0, p)),
+            pl.BlockSpec((1, 2, rows), lambda p: (p, 0, 0)),
+        ],
+        out_shape=[
+            jax.ShapeDtypeStruct((rows, cols), BF),
+            jax.ShapeDtypeStruct((rows, pairs * 128), BF),
+            jax.ShapeDtypeStruct((pairs, 2, rows), F32),
+        ],
+        cost_estimate=pl.CostEstimate(
+            flops=pairs * 2 * rows * rows * 64 * 4,
+            transcendentals=pairs * 2 * rows * rows,
+            bytes_accessed=rows * cols * 8,
+        ),
+        compiler_params=pltpu.CompilerParams(vmem_limit_bytes=48 << 20),
+        name="attend",
+    )(mixed, cos_wide, sin_wide, seg_col, seg_row)
+
+
+def attend_back(qkv, grad_att, lse, cos_wide, sin_wide, seg_col, seg_row):
+    rows, cols = qkv.shape
+    pairs = cols // 384
+    whole = lambda p: (0, 0)
+    return pl.pallas_call(
+        attend_back_kernel,
+        grid=(pairs,),
+        in_specs=[
+            pl.BlockSpec((rows, 384), lambda p: (0, p)),
+            pl.BlockSpec((rows, 128), lambda p: (0, p)),
+            pl.BlockSpec((1, 2, rows), lambda p: (p, 0, 0)),
+            pl.BlockSpec((rows, 384), whole),
+            pl.BlockSpec((rows, 384), whole),
+            pl.BlockSpec((rows, 1), whole),
+            pl.BlockSpec((1, rows), whole),
+        ],
+        out_specs=pl.BlockSpec((rows, 384), lambda p: (0, p)),
+        out_shape=jax.ShapeDtypeStruct((rows, cols), BF),
+        scratch_shapes=[VM((rows, 384), F32)],
+        cost_estimate=pl.CostEstimate(
+            flops=pairs * 2 * rows * rows * 64 * 10,
+            transcendentals=pairs * 2 * rows * rows,
+            bytes_accessed=rows * cols * 8,
+        ),
+        compiler_params=pltpu.CompilerParams(vmem_limit_bytes=48 << 20),
+        name="attend_back",
+    )(qkv, grad_att, lse, cos_wide, sin_wide, seg_col, seg_row)
+
+
+def remote(source, target, send_sem, recv_sem, device):
+    return pltpu.make_async_remote_copy(
+        src_ref=source, dst_ref=target, send_sem=send_sem, recv_sem=recv_sem,
+        device_id=device, device_id_type=MESH_ID,
+    )
+
+
+def greet(peers):
+    barrier = pltpu.get_barrier_semaphore()
+    for peer in peers:
+        pl.semaphore_signal(barrier, inc=1, device_id=peer, device_id_type=MESH_ID)
+    pl.semaphore_wait(barrier, len(peers))
+
+
+def near_peers():
+    dp, mine = lax.axis_index("dp"), lax.axis_index("tensor")
+    across = (mine + 2) % 4
+    beside = mine + 1 - 2 * (mine % 2)
+    return dp, mine, across, beside
+
+
+def far_peers():
+    dp, mine = lax.axis_index("dp"), lax.axis_index("tensor")
+    level, side = dp // 2, dp % 2
+    cross = dp + 1 - 2 * side
+    ahead = [((level + k) % 4) * 2 + side for k in range(4)]
+    behind = [((level + 4 - k) % 4) * 2 + side for k in range(4)]
+    return dp, mine, cross, ahead, behind
+
+
+class RowGather:
+    sems = [DMA((SPLIT,)), DMA((SPLIT,)), DMA((SPLIT + 1,)), DMA((SPLIT + 1,)), DMA]
+
+    def __init__(self, source, target, sems):
+        self.source, self.target, self.sems_in = source, target, sems
+        self.rows = source.shape[0]
+
+    def start(self):
+        dp, mine, across, beside = near_peers()
+        send_y, recv_y, send_c, recv_c, own = self.sems_in
+        rows, part = self.rows, self.rows // SPLIT
+        self.links = []
+        for j in range(SPLIT):
+            link = remote(
+                self.source.at[pl.ds(j * part, part)],
+                self.target.at[pl.ds(mine * rows + j * part, part)],
+                send_y.at[j], recv_y.at[j], (dp, across))
+            link.start()
+            self.links.append(link)
+        self.beside = remote(
+            self.source, self.target.at[pl.ds(mine * rows, rows)],
+            send_c.at[SPLIT], recv_c.at[SPLIT], (dp, beside))
+        self.beside.start()
+        self.local = pltpu.make_async_copy(
+            self.source, self.target.at[pl.ds(mine * rows, rows)], own)
+        self.local.start()
+        self.forwards = []
+
+    def step(self, j):
+        dp, mine, across, beside = near_peers()
+        send_y, recv_y, send_c, recv_c, own = self.sems_in
+        rows, part = self.rows, self.rows // SPLIT
+        place = self.target.at[pl.ds(across * rows + j * part, part)]
+        remote(self.source.at[pl.ds(j * part, part)], place,
+               send_y.at[j], recv_y.at[j], (dp, across)).wait_recv()
+        forward = remote(place, place, send_c.at[j], recv_c.at[j], (dp, beside))
+        forward.start()
+        self.forwards.append(forward)
+
+    def finish(self):
+        dp, mine, across, beside = near_peers()
+        send_y, recv_y, send_c, recv_c, own = self.sems_in
+        rows, part = self.rows, self.rows // SPLIT
+        other = beside
+        remote(self.source, self.target.at[pl.ds(other * rows, rows)],
+               send_c.at[SPLIT], recv_c.at[SPLIT], (dp, beside)).wait_recv()
+        diagonal = (beside + 2) % 4
+        for j in range(SPLIT):
+            place = self.target.at[pl.ds(diagonal * rows + j * part, part)]
+            remote(place, place, send_c.at[j], recv_c.at[j], (dp, beside)).wait_recv()
+        for link in self.links + self.forwards + [self.beside]:
+            link.wait_send()
+        self.local.wait()
+
+
+class WeightGather:
+    sems = [DMA((8,)), DMA((8,)), DMA]
+
+    def __init__(self, source, target, sems, axis):
+        self.source, self.target, self.sems_in, self.axis = source, target, sems, axis
+
+    def place(self, index):
+        size = self.source.shape[self.axis]
+        window = pl.ds(pl.multiple_of(index * size, size), size)
+        return self.target.at[window] if self.axis == 0 else self.target.at[:, window]
+
+    def start(self):
+        dp, mine, cross, ahead, behind = far_peers()
+        send, recv, own = self.sems_in
+        self.links = []
+        for k in (2, 1, 3):
+            link = remote(self.source, self.place(dp), send.at[k], recv.at[k], (ahead[k], mine))
+            link.start()
+            self.links.append(link)
+        link = remote(self.source, self.place(dp), send.at[4], recv.at[4], (cross, mine))
+        link.start()
+        self.links.append(link)
+        self.local = pltpu.make_async_copy(self.source, self.place(dp), own)
+        self.local.start()
+
+    def step(self, k):
+        dp, mine, cross, ahead, behind = far_peers()
+        send, recv, own = self.sems_in
+        place = self.place(behind[k])
+        remote(self.source, place, send.at[k], recv.at[k], (ahead[k], mine)).wait_recv()
+        link = remote(place, place, send.at[4 + k], recv.at[4 + k], (cross, mine))
+        link.start()
+        self.links.append(link)
+
+    def finish(self):
+        dp, mine, cross, ahead, behind = far_peers()
+        send, recv, own = self.sems_in
+        for k in range(4):
+            index = behind[k] + 1 - 2 * (dp % 2)
+            place = self.place(index)
+            remote(place, place, send.at[4 + k], recv.at[4 + k], (cross, mine)).wait_recv()
+        for link in self.links:
+            link.wait_send()
+        self.local.wait()
+
+
+class RowReduce:
+    sems = [DMA((SPLIT + 1,)), DMA((SPLIT + 1,)), DMA((SPLIT,)), DMA((SPLIT,))]
+
+    @staticmethod
+    def scratch(rows, width):
+        return [VM((rows, width), BF), VM((rows, width), BF), VM((rows, width), BF), VM((rows, width), BF)]
+
+    def __init__(self, source, target, scratch, sems):
+        self.source, self.target, self.scratch_in, self.sems_in = source, target, scratch, sems
+        self.rows = target.shape[0]
+
+    def start(self):
+        dp, mine, across, beside = near_peers()
+        send_c, recv_c, send_y, recv_y = self.sems_in
+        far_in, near_in, sums, y_in = self.scratch_in
+        rows, part = self.rows, self.rows // SPLIT
+        diagonal = (beside + 2) % 4
+        self.links = []
+        for j in range(SPLIT):
+            link = remote(
+                self.source.at[pl.ds(diagonal * rows + j * part, part)],
+                far_in.at[pl.ds(j * part, part)], send_c.at[j], recv_c.at[j], (dp, beside))
+            link.start()
+            self.links.append(link)
+        link = remote(
+            self.source.at[pl.ds(beside * rows, rows)], near_in,
+            send_c.at[SPLIT], recv_c.at[SPLIT], (dp, beside))
+        link.start()
+        self.links.append(link)
+
+    def step(self, j):
+        dp, mine, across, beside = near_peers()
+        send_c, recv_c, send_y, recv_y = self.sems_in
+        far_in, near_in, sums, y_in = self.scratch_in
+        rows, part = self.rows, self.rows // SPLIT
+        window = pl.ds(j * part, part)
+        self.links[j].wait_recv()
+        sums[window] = (
+            self.source[pl.ds(across * rows + j * part, part)].astype(F32)
+            + far_in[window].astype(F32)
+        ).astype(BF)
+        link = remote(sums.at[window], y_in.at[window], send_y.at[j], recv_y.at[j], (dp, across))
+        link.start()
+        self.links.append(link)
+
+    def finish(self):
+        dp, mine, across, beside = near_peers()
+        far_in, near_in, sums, y_in = self.scratch_in
+        rows, part = self.rows, self.rows // SPLIT
+        self.links[SPLIT].wait_recv()
+        for j in range(SPLIT):
+            window = pl.ds(j * part, part)
+            self.links[SPLIT + 1 + j].wait_recv()
+            self.target[window] = (
+                self.source[pl.ds(mine * rows + j * part, part)].astype(F32)
+                + near_in[window].astype(F32)
+                + y_in[window].astype(F32)
+            )
+        for link in self.links:
+            link.wait_send()
+
+
+class WeightReduce:
+    sems = [DMA((8,)), DMA((8,))]
+
+    @staticmethod
+    def scratch(shape):
+        return [VM((4, *shape), BF), VM((4, *shape), BF), VM((4, *shape), BF)]
+
+    def __init__(self, source, target, scratch, sems, axis):
+        self.source, self.target, self.scratch_in, self.sems_in = source, target, scratch, sems
+        self.axis = axis
+
+    def window(self, index):
+        size = self.target.shape[self.axis]
+        window = pl.ds(pl.multiple_of(index * size, size), size)
+        return (window,) if self.axis == 0 else (slice(None), window)
+
+    def start(self):
+        dp, mine, cross, ahead, behind = far_peers()
+        send, recv = self.sems_in
+        x_in, sums, z_in = self.scratch_in
+        self.links = {}
+        for k in (2, 1, 3, 0):
+            index = ahead[k] + 1 - 2 * (dp % 2)
+            link = remote(self.source.at[self.window(index)], x_in.at[k],
+                          send.at[k], recv.at[k], (cross, mine))
+            link.start()
+            self.links[k] = link
+
+    def step(self, k):
+        dp, mine, cross, ahead, behind = far_peers()
+        send, recv = self.sems_in
+        x_in, sums, z_in = self.scratch_in
+        self.links[k].wait_recv()
+        sums[k] = (self.source[self.window(ahead[k])].astype(F32) + x_in[k].astype(F32)).astype(BF)
+        if k:
+            link = remote(sums.at[k], z_in.at[k], send.at[4 + k], recv.at[4 + k], (ahead[k], mine))
+            link.start()
+            self.links[4 + k] = link
+
+    def finish(self):
+        x_in, sums, z_in = self.scratch_in
+        for k in (1, 2, 3):
+            self.links[4 + k].wait_recv()
+        self.target[...] = (
+            sums[0].astype(F32) + z_in[1].astype(F32) + z_in[2].astype(F32) + z_in[3].astype(F32)
+        )
+        for link in self.links.values():
+            link.wait_send()
+
+
+def run_parts(near, far):
+    dp, mine, across, beside = near_peers()
+    peers = [(dp, across), (dp, beside)] if near else []
+    if far:
+        dp, mine, cross, ahead, behind = far_peers()
+        peers += [(cross, mine)] + [(ahead[k], mine) for k in (1, 2, 3)]
+    greet(peers)
+    for part in near + far:
+        part.start()
+    for j in range(SPLIT):
+        for part in near:
+            part.step(j)
+        for part in far:
+            k = (2, 1, 3, 0)[j]
+            if k or isinstance(part, WeightReduce):
+                part.step(k)
+    for part in near + far:
+        part.finish()
+
+
+def comm_call(kernel, args, outs, out_spaces, scratch, ident, name):
+    return pl.pallas_call(
+        kernel,
+        out_shape=[jax.ShapeDtypeStruct(*out) for out in outs],
+        in_specs=[pl.BlockSpec(memory_space=VM)] * len(args),
+        out_specs=[pl.BlockSpec(memory_space=space) for space in out_spaces],
+        scratch_shapes=scratch,
+        compiler_params=pltpu.CompilerParams(
+            collective_id=ident, has_side_effects=True, vmem_limit_bytes=40 << 20
+        ),
+        name=name,
+    )(*args)
+
+
+def gather_rows(ident, *arrays):
+    count = len(arrays)
+    per = len(RowGather.sems)
+
+    def kernel(*refs):
+        sems = refs[2 * count :]
+        run_parts(
+            [RowGather(refs[i], refs[count + i], sems[i * per : (i + 1) * per]) for i in range(count)], []
+        )
+
+    return comm_call(
+        kernel, arrays, [((4 * a.shape[0], a.shape[1]), BF) for a in arrays],
+        [pl.ANY] * count, RowGather.sems * count, ident, "gather_rows")
+
+
+def gather_first(ident, rows, weights, axes):
+    count = 1 + len(weights)
+    per_row, per_weight = len(RowGather.sems), len(WeightGather.sems)
+
+    def kernel(*refs):
+        ins, outs, sems = refs[:count], refs[count : 2 * count], refs[2 * count :]
+        near = [RowGather(ins[0], outs[0], sems[:per_row])]
+        sems = sems[per_row:]
+        far = [
+            WeightGather(ins[1 + i], outs[1 + i], sems[i * per_weight : (i + 1) * per_weight], axes[i])
+            for i in range(len(weights))
+        ]
+        run_parts(near, far)
+
+    shapes = [((4 * rows.shape[0], rows.shape[1]), BF)]
+    for weight, axis in zip(weights, axes):
+        shape = list(weight.shape)
+        shape[axis] = shape[axis] * 8
+        shapes.append((tuple(shape), BF))
+    return comm_call(
+        kernel, (rows, *weights), shapes, [pl.ANY] * count,
+        RowGather.sems + WeightGather.sems * len(weights), ident, "gather_first")
+
+
+def reduce_sums(ident, partial, grads, axes):
+    rows = partial.shape[0] // 4
+    count = 1 + len(grads)
+    shapes = [((rows, partial.shape[1]), F32)]
+    scratch = RowReduce.scratch(rows, partial.shape[1]) + RowReduce.sems
+    for grad, axis in zip(grads, axes):
+        shape = list(grad.shape)
+        shape[axis] = shape[axis] // 8
+        shapes.append((tuple(shape), F32))
+        scratch = scratch + WeightReduce.scratch(tuple(shape)) + WeightReduce.sems
+
+    def kernel(*refs):
+        ins, outs, rest = refs[:count], refs[count : 2 * count], refs[2 * count :]
+        near = [RowReduce(ins[0], outs[0], rest[:4], rest[4:8])]
+        far = []
+        for i in range(len(grads)):
+            mine = rest[8 + 5 * i : 13 + 5 * i]
+            far.append(WeightReduce(ins[1 + i], outs[1 + i], mine[:3], mine[3:], axes[i]))
+        run_parts(near, far)
+
+    return comm_call(kernel, (partial, *grads), shapes, [VM] * count, scratch, ident, "reduce_sums")
+
+
+def sum_gains_kernel(part_ref, out_ref, near_in, mid, far_in, send_n, recv_n, send_f, recv_f):
+    dp, mine = lax.axis_index("dp"), lax.axis_index("tensor")
+    near = [(dp, (mine + k) % 4) for k in range(1, 4)]
+    far = [((dp + k) % 8, mine) for k in range(1, 8)]
+    greet(near + far)
+    links = []
+    for k in range(3):
+        link = remote(part_ref, near_in.at[k], send_n.at[k], recv_n.at[k], near[k])
+        link.start()
+        links.append(link)
+    for link in links:
+        link.wait_recv()
+    mid[...] = part_ref[...] + near_in[0] + near_in[1] + near_in[2]
+    more = []
+    for k in range(7):
+        link = remote(mid, far_in.at[k], send_f.at[k], recv_f.at[k], far[k])
+        link.start()
+        more.append(link)
+    total = mid[...]
+    for k in range(7):
+        more[k].wait_recv()
+        total = total + far_in[k]
+    out_ref[...] = total
+    for link in links + more:
+        link.wait_send()
+
+
+def sum_gains(ident, parts):
+    shape = parts.shape
+    return comm_call(
+        sum_gains_kernel, (parts,), [(shape, F32)], [VM],
+        [VM((3, *shape), F32), VM(shape, F32), VM((7, *shape), F32),
+         DMA((3,)), DMA((3,)), DMA((7,)), DMA((7,))], ident, "sum_gains")[0]
 
 
 def layer_norm(row_data, norm_gain):
@@ -304,7 +820,95 @@
     )
 
 
+def fast_body(
+    tokens,
+    attn_gain,
+    qkv_weight,
+    out_weight,
+    mlp_gain,
+    in_weight,
+    down_weight,
+    seg_lengths,
+    cotangent,
+):
+    tok_dev, model_width = tokens.shape
+    pack_rows = tok_dev * 4
+    heads_local = qkv_weight.shape[1]
+    head_dim = qkv_weight.shape[2] // 3
+    hidden_local = in_weight.shape[2]
+    row_data = tokens.astype(F32)
+    normed_attn, unit_attn, inverse_attn = layer_norm(row_data, attn_gain)
+    in_full = lax.all_gather(in_weight, "dp", axis=0, tiled=True)
+    down_full = lax.all_gather(down_weight, "dp", axis=1, tiled=True)
+    attn_input, qkv_flat, out_full = gather_first(
+        1,
+        normed_attn.astype(BF),
+        (qkv_weight.reshape(qkv_weight.shape[0], heads_local * 3 * head_dim), out_weight),
+        (0, 1),
+    )
+    seg_ids, position = segment_info(seg_lengths[0], pack_rows)
+    cos_table, sin_table = rotary(position, head_dim)
+    ones, zeros = jnp.ones((pack_rows, head_dim), F32), jnp.zeros((pack_rows, head_dim), F32)
+    cos_wide = jnp.concatenate([cos_table] * 4 + [ones] + [cos_table] * 4 + [ones], axis=1)
+    sin_wide = jnp.concatenate(([-sin_table, sin_table] * 2 + [zeros]) * 2, axis=1)
+    seg_col, seg_row = seg_ids[:, None], seg_ids[None, :]
+    mixed_proj = dot_plain(attn_input, qkv_flat)
+    qkv_rows, attended, log_totals = attend(mixed_proj, cos_wide, sin_wide, seg_col, seg_row)
+    residual = row_data + reduce_sums(2, dot_plain(attended, out_full).astype(BF), (), ())[0]
+    normed_mlp, unit_mlp, inverse_mlp = layer_norm(residual, mlp_gain)
+    mlp_rows, cotangent_rows = gather_rows(3, normed_mlp.astype(BF), cotangent)
+    in_flat = in_full.reshape(model_width, -1)
+    lifted = dot_plain(mlp_rows, in_flat)
+    gate = lifted[:, hidden_local:]
+    act_gelu, act_slope = gelu_parts(lifted[:, :hidden_local])
+    activated = (act_gelu * gate).astype(BF)
+    grad_act = dot_last(cotangent_rows, down_full)
+    grad_lifted = jnp.concatenate(
+        [grad_act * gate * act_slope, grad_act * act_gelu], axis=1
+    ).astype(BF)
+    grad_mlp_in = reduce_sums(4, dot_last(grad_lifted, in_flat).astype(BF), (), ())[0]
+    layer_sum = lax.psum_scatter(
+        dot_plain(activated, down_full).astype(BF), "tensor", scatter_dimension=0, tiled=True
+    )
+    layer_out = (residual + layer_sum.astype(F32)).astype(BF)
+    grad_in_part = dot_first(mlp_rows, grad_lifted).reshape(in_full.shape)
+    grad_down_part = dot_first(activated, cotangent_rows)
+    in_grad = lax.psum_scatter(
+        grad_in_part.astype(BF), "dp", scatter_dimension=0, tiled=True
+    ).astype(F32)
+    down_grad = lax.psum_scatter(
+        grad_down_part.astype(BF), "dp", scatter_dimension=1, tiled=True
+    ).astype(F32)
+    grad_resid_norm, mlp_gain_part = norm_back(grad_mlp_in, unit_mlp, inverse_mlp, mlp_gain)
+    grad_residual = cotangent.astype(F32) + grad_resid_norm
+    grad_branch = gather_rows(5, grad_residual.astype(BF))[0]
+    grad_out_part = dot_first(attended, grad_branch).astype(BF)
+    grad_attended = dot_last(grad_branch, out_full).astype(BF)
+    grad_mixed = attend_back(
+        qkv_rows, grad_attended, log_totals, cos_wide, sin_wide, seg_col, seg_row
+    )
+    grad_qkv_part = dot_first(attn_input, grad_mixed).astype(BF)
+    grad_attn_in, qkv_grad, out_grad = reduce_sums(
+        6, dot_last(grad_mixed, qkv_flat).astype(BF), (grad_qkv_part, grad_out_part), (0, 1)
+    )
+    grad_rows_attn, attn_gain_part = norm_back(grad_attn_in, unit_attn, inverse_attn, attn_gain)
+    grad_tokens = (grad_residual + grad_rows_attn).astype(BF)
+    gains = sum_gains(7, jnp.concatenate([attn_gain_part[None], mlp_gain_part[None], jnp.zeros((6, model_width), F32)]))
+    return (
+        layer_out,
+        grad_tokens,
+        gains[0],
+        qkv_grad.reshape(qkv_weight.shape),
+        out_grad,
+        gains[1],
+        in_grad,
+        down_grad,
+    )
+
+
 def solution(mesh):
+    fast = mesh.shape["tensor"] == 4 and mesh.shape["dp"] == 8
+    chosen = fast_body if fast else body
     in_specs = (
         P(("dp", "tensor"), None),
         P(),
@@ -326,4 +930,4 @@
         P("dp", None, "tensor"),
         P("tensor", "dp"),
     )
-    return jax.shard_map(body, mesh=mesh, in_specs=in_specs, out_specs=out_specs, check_vma=False)
+    return jax.shard_map(chosen, mesh=mesh, in_specs=in_specs, out_specs=out_specs, check_vma=False)

time: 736 us -> 407 us (0.55)
  waiting for transfers between devices: 382 us -> 55 us
  Pallas kernels: 0 us -> 239 us
  matrix products: 169 us -> 44.2 us
  blocking collectives: 70.2 us -> 0 us
  local copies, waits for them, and re-layouts: 51.6 us -> 30.7 us
  other arithmetic: 31.6 us -> 15.8 us
    pallas_call x0 -> x9, Pallas kernels: none -> 239 us  [the longest x7 192 us: comm_call(): pl.pallas_call(kernel, out_shape=[jax.ShapeDtypeStruct(*out) for out in o...]
    all_gather x7 -> x2, waiting for transfers between devices: 179 us -> 0.01 us  [the longest x1 0.01 us: fast_body(): in_full = lax.all_gather(in_weight, 'dp', axis=0, tiled=True)]
    dot_general x14 -> x0, matrix products: 112 us -> none  [the longest x2 46.3 us: block_step(): jnp.einsum('hqk,qhd->khd', grad_scores, query_part, preferred_element_typ...]
    unnamed x19 -> x7, waiting for transfers between devices: 109 us -> 23.9 us
    reduce_scatter x4 -> x1, waiting for transfers between devices: 93.5 us -> 31.1 us  [fast_body(): lax.psum_scatter(dot_plain(activated, down_full).astype(BF), 'tensor', sc...]
    psum x1 -> x0, blocking collectives: 39.5 us -> none  [body(): lax.psum((attn_gain_part, mlp_gain_part), ('dp', 'tensor'))]
    all_gather x1 -> x0, blocking collectives: 30.7 us -> none  [body(): lax.all_gather(out_weight, 'dp', axis=1, tiled=True)]
    dynamic_update_slice x4 -> x0, local copies, waits for them, and re-layouts: 23.8 us -> none  [attention_forward(): lax.map(one_block, jnp.arange(block_count, dtype=jnp.int32))]
  transfers between devices with their start and end apart: 15 -> 5, of which waited for: 12 -> 2; matrix products, arithmetic and copies ran while one was open for 28% -> 17% of each run, Pallas kernels for 0% -> 60%
where the time goes in v1:
time: 407 us; the launch traced here: 400 us
  Pallas kernels  239 us (59%)
  waiting for transfers between devices  55 us (14%)
  matrix products  44.2 us (11%)
  local copies, waits for them, and re-layouts  30.7 us (8%)
  other arithmetic  15.8 us (4%)
  between operations  14.7 us (4%)
    pallas_call x7, Pallas kernels, comm_call(): pl.pallas_call(kernel, out_shape=[jax.ShapeDtypeStruct(*out) for out in o...  192 us
    reduce_scatter x1, waiting for transfers between devices, fast_body(): lax.psum_scatter(dot_plain(activated, down_full).astype(BF), 'tensor', sc...  31.1 us
    pallas_call x1, Pallas kernels, attend_back(): pl.pallas_call(attend_back_kernel, grid=(pairs,), in_specs=[pl.BlockSpec(...  25.4 us
    unnamed x7, waiting for transfers between devices  23.9 us
    pallas_call x1, Pallas kernels, attend(): pl.pallas_call(attend_kernel, grid=(pairs,), in_specs=[pl.BlockSpec((rows...  22.1 us
    unnamed x53, local copies, waits for them, and re-layouts  18.3 us
    dot_general x4, matrix products, dot_plain(): return jnp.dot(left, right, preferred_element_type=jnp.float32)  16.8 us
    dot_general x4, matrix products, dot_last(): lax.dot_general(left, right, (((1,), (1,)), ((), ())), preferred_element_...  16.6 us
  transfers between devices with their start and end apart: 5, of which 2 were waited for; matrix products, arithmetic and copies ran while one was open for 17% of the time, Pallas kernels for 60%

profile of v1, /device:TPU:0, one launch (start us, length us, event | category | flops | bytes accessed | tf_op | source)
XLA Modules:
  0.0 399.8 jit_solution(5040610732407639265)
XLA Ops:
  7.2 0.7 all-gather.3.cloned.1.call-update
  8.0 0.7 all-gather.5.cloned.1.call-update
  8.7 1.2 convert_reduce_fusion
  9.9 1.3 fusion.18
  11.3 1.1 copy.31.refs_1_
  12.3 0.8 reduce-window.8
  13.2 0.7 convert_reduce_fusion.1
  13.9 1.0 fusion.11.refs_0_
  14.9 62.5 %gather_first.1 = (bf16[1024,1024]{1,0:T(8,128)(2,1)S(1)}, bf16[1024,768]{1,0:T(8,128)(2,1)S(1)}, bf16[256,1024]{1,0:T(8,128)(2,1)S(1)}) custom-call(bf16[256,1024]{1,0:T(8,128)(2,1)S(1)} %fusion.11.refs_0_, bf16[128,768]{1,0:T(8,128)(2,1)S(1)} %copy.31.refs_1_, bf16[256,128]{1,0:T(8,128)(2,1)S(1)} %copy-done.4), custom_call_target="tpu_custom_call" | custom-call | tf_op jit(solution)/shard_map/gather_first/pallas_call | solution.py:437
  77.5 3.4 fusion.25.mixed_ref
  81.0 3.0 multiply_sine_fusion
  84.0 0.2 copy.33.segc_ref
  84.2 0.8 broadcast_in_dim.54
  85.1 3.2 concatenate.13.cos_ref
  88.3 5.4 %concatenate.14.sin_ref = f32[1024,384]{1,0:T(8,128)} concatenate(f32[1024,32]{1,0:T(8,128)} %get-tuple-element.57, f32[1024,32]{1,0:T(8,128)} %get-tuple-element.56, f32[1024,32]{1,0:T(8,128)} %get-tuple-element.57, f32[1024,32]{1,0:T(8,128)} %get-tuple-element.56, f32[1024,64]{1,0:T(8,128)S(1)} %broadcast_in_dim.55, f32[1024,32]{1,0:T(8,128)} %get-tuple-element.57, ...), dimensions={1} | concatenate | bytes 3145728 | tf_op jit(solution)/shard_map/concatenate | solution.py:853
  93.8 1.4 copy-done.3
  95.2 22.1 %attend.1 = (bf16[1024,768]{1,0:T(8,128)(2,1)S(1)}, bf16[1024,256]{1,0:T(8,128)(2,1)S(1)}, f32[2,2,1024]{2,1,0:T(2,128)S(1)}) custom-call(f32[1024,768]{1,0:T(8,128)} %fusion.25.mixed_ref, f32[1024,384]{1,0:T(8,128)S(1)} %concatenate.13.cos_ref, f32[1024,384]{1,0:T(8,128)S(1)} %copy-done.3, s32[1024,1]{1,0:T(8,128)S(1)} %copy.33.segc_ref, s32[1,1024]{1,0:T(1,128)S(1)} %bitcast.42), custom_call_target="tpu_custom_call" | custom-call | flops 1073741824 | bytes 6291456 | tf_op jit(solution)/shard_map/attend/pallas_call | solution.py:114
  117.2 0.7 convolution_convert_fusion.2.refs_0_
  118.0 15.9 %reduce_sums.3 = f32[256,1024]{1,0:T(8,128)S(1)} custom-call(bf16[1024,1024]{1,0:T(8,128)(2,1)S(1)} %convolution_convert_fusion.2.refs_0_), custom_call_target="tpu_custom_call" | custom-call | tf_op jit(solution)/shard_map/reduce_sums/pallas_call | solution.py:437
  134.0 0.2 fusion.23
  134.2 0.2 multiply_reduce_fusion.2
  134.4 0.7 copy-done.14
  135.1 0.2 multiply_convert_fusion.2.refs_0_
  135.4 26.3 %gather_rows.2 = (bf16[1024,1024]{1,0:T(8,128)(2,1)S(1)}, bf16[1024,1024]{1,0:T(8,128)(2,1)S(1)}) custom-call(bf16[256,1024]{1,0:T(8,128)(2,1)S(1)} %multiply_convert_fusion.2.refs_0_, bf16[256,1024]{1,0:T(8,128)(2,1)S(1)} %copy-done), custom_call_target="tpu_custom_call" | custom-call | tf_op jit(solution)/shard_map/gather_rows/pallas_call | solution.py:437
  161.7 1.3 copy-done.7
  163.0 1.4 copy-done.8
  164.4 7.7 %fusion.26 = f32[1024,1312]{0,1:T(8,128)} fusion(bf16[1024,1024]{1,0:T(8,128)(2,1)} %copy-done.7, bf16[1024,1312]{0,1:T(8,128)(2,1)} %bitcast.56), kind=kOutput, calls=%fused_computation.69 | convolution fusion | flops 2751463424 | bytes 10158080 | tf_op jit(solution)/shard_map/dot_general | solution.py:18
  172.1 7.9 %fusion.4 = (bf16[1024,656]{0,1:T(8,128)(2,1)}, bf16[1024,656]{0,1:T(8,128)(2,1)}, bf16[1024,656]{0,1:T(8,128)(2,1)S(1)}) fusion(f32[1024,1312]{0,1:T(8,128)} %fusion.26, bf16[1024,1024]{1,0:T(8,128)(2,1)} %copy-done.8, bf16[656,1024]{1,0:T(8,128)(2,1)} %all-gather.5.cloned.1.call-done), kind=kOutput, calls=%fused_computation.6 | convolution fusion | flops 1386479616 | bytes 12845056 | tf_op jit(solution)/shard_map/dot_general | solution.py:28
  180.0 1.1 copy-done.22
  181.1 1.6 convolution_convert_fusion.6
  182.6 1.6 copy.38
  184.3 0.0 reduce-scatter.8.cloned.1.call-start
  184.3 4.9 %convolution_convert_fusion.4 = bf16[1024,1024]{1,0:T(8,128)(2,1)} fusion(bf16[1024,656]{0,1:T(8,128)(2,1)} %copy-done.22, bf16[656,1024]{1,0:T(8,128)(2,1)} %all-gather.5.cloned.1.call-done), kind=kOutput, calls=%fused_computation.15 | convolution fusion | flops 1376780288 | bytes 4784128 | tf_op jit(solution)/shard_map/dot_general | solution.py:18
  189.3 1.3 copy-done.23
  190.6 6.5 %convolution_convert_fusion = bf16[1024,1312]{0,1:T(8,128)(2,1)} fusion(bf16[1024,1024]{1,0:T(8,128)(2,1)} %copy-done.7, bf16[1024,656]{0,1:T(8,128)(2,1)} %get-tuple-element.51, bf16[1024,656]{0,1:T(8,128)(2,1)S(1)} %copy-done.23), kind=kOutput, calls=%fused_computation.1 | convolution fusion | flops 2758180864 | bytes 7471104 | tf_op jit(solution)/shard_map/dot_general | solution.py:22
  197.1 4.7 %copy.40 = bf16[1024,1312]{1,0:T(8,128)(2,1)} copy(bf16[1024,1312]{0,1:T(8,128)(2,1)} %convolution_convert_fusion) | data formatting | bytes 5373952
  201.9 0.1 pad.2.clone
  201.9 6.2 %convolution_convert_fusion.1.refs_0_ = bf16[1024,1024]{1,0:T(8,128)(2,1)S(1)} fusion(bf16[1024,1312]{0,1:T(8,128)(2,1)} %bitcast.57, bf16[1024,656]{0,1:T(8,128)(2,1)} %get-tuple-element.51, bf16[1024,656]{0,1:T(8,128)(2,1)} %get-tuple-element.50), kind=kOutput, calls=%fused_computation.12 | convolution fusion | flops 2757885952 | bytes 7471104 | tf_op jit(solution)/shard_map/dot_general | solution.py:28
  208.1 15.8 %reduce_sums.4 = f32[256,1024]{1,0:T(8,128)S(1)} custom-call(bf16[1024,1024]{1,0:T(8,128)(2,1)S(1)} %convolution_convert_fusion.1.refs_0_), custom_call_target="tpu_custom_call" | custom-call | tf_op jit(solution)/shard_map/reduce_sums/pallas_call | solution.py:437
  223.9 0.5 multiply_reduce_fusion
  224.5 22.5 %reduce-scatter.12.cloned.1.call-done = bf16[128,656]{1,0:T(8,128)(2,1)} async-done(((bf16[1024,656]{1,0:T(8,128)(2,1)}), bf16[128,656]{1,0:T(8,128)(2,1)}) %reduce-scatter.12.cloned.1.call-update) | async-done | bytes 167952
  246.9 1.1 copy.39
  248.0 0.8 convert_element_type.96
  248.8 31.1 %reduce-scatter.8.cloned.1.call-done = bf16[256,1024]{1,0:T(8,128)(2,1)} async-done(((bf16[1024,1024]{1,0:T(8,128)(2,1)}), bf16[256,1024]{1,0:T(8,128)(2,1)}) %reduce-scatter.8.cloned.1.call-update) | async-done | bytes 524304 | tf_op jit(solution)/shard_map/reduce_scatter | solution.py:870
  279.8 3.0 fusion.22
  282.8 14.8 %gather_rows.3 = bf16[1024,1024]{1,0:T(8,128)(2,1)S(1)} custom-call(bf16[256,1024]{1,0:T(8,128)(2,1)S(1)} %get-tuple-element.46.refs_0_), custom_call_target="tpu_custom_call" | custom-call | tf_op jit(solution)/shard_map/gather_rows/pallas_call | solution.py:437
  297.7 0.7 convolution_convert_fusion.8.ga_ref
  298.4 0.7 copy-done.2
  299.1 0.5 copy-done.13
  299.5 25.4 %attend_back.1 = bf16[1024,768]{1,0:T(8,128)(2,1)S(1)} custom-call(bf16[1024,768]{1,0:T(8,128)(2,1)S(1)} %copy-done.13, bf16[1024,256]{1,0:T(8,128)(2,1)S(1)} %convolution_convert_fusion.8.ga_ref, f32[2,2,1024]{2,1,0:T(2,128)S(1)} %get-tuple-element.26.lse_ref, f32[1024,384]{1,0:T(8,128)S(1)} %copy-done.2, f32[1024,384]{1,0:T(8,128)} %concatenate.14.sin_ref, ...), custom_call_target="tpu_custom_call" | custom-call | flops 2684354560 | bytes 6291456 | tf_op jit(solution)/shard_map/attend_back/pallas_call | solution.py:148
  325.0 0.7 convolution_convert_fusion.7.refs_2_
  325.7 0.7 copy-done.11
  326.4 1.8 convolution_convert_fusion.3.refs_0_
  328.2 1.9 convolution_convert_fusion.5.refs_1_
  330.2 44.7 %reduce_sums.5 = (f32[256,1024]{1,0:T(8,128)S(1)}, f32[128,768]{1,0:T(8,128)S(1)}, f32[256,128]{1,0:T(8,128)S(1)}) custom-call(bf16[1024,1024]{1,0:T(8,128)(2,1)S(1)} %convolution_convert_fusion.3.refs_0_, bf16[1024,768]{1,0:T(8,128)(2,1)S(1)} %convolution_convert_fusion.5.refs_1_, bf16[256,1024]{1,0:T(8,128)(2,1)S(1)} %convolution_convert_fusion.7.refs_2_), custom_call_target="tpu_custom_call" | custom-call | tf_op jit(solution)/shard_map/reduce_sums/pallas_call | solution.py:437
  374.9 0.6 fusion.17
  375.5 0.1 maximum_maximum_fusion.part_ref
  375.6 11.7 %sum_gains.1 = f32[8,1024]{1,0:T(8,128)S(1)} custom-call(f32[8,1024]{1,0:T(8,128)S(1)} %maximum_maximum_fusion.part_ref), custom_call_target="tpu_custom_call" | custom-call | tf_op jit(solution)/shard_map/sum_gains/pallas_call | solution.py:437
  387.3 0.9 copy.35
  388.2 0.6 fusion.24
  388.8 1.2 fusion.16
  390.1 1.2 copy.41
  391.3 0.9 convert_element_type.94
  392.1 0.7 copy.43
  (60 shorter events, 0.4 us)
Async XLA Ops:
  7.2 6.8 %copy-start.16 = (bf16[256,1024]{1,0:T(8,128)(2,1)S(1)}, bf16[256,1024]{1,0:T(8,128)(2,1)}, u32[]{:S(2)}) copy-start(bf16[256,1024]{1,0:T(8,128)(2,1)} %param.9) | copy-start | bytes 1572868
  7.2 7.7 %copy-start.4 = (bf16[256,128]{1,0:T(8,128)(2,1)S(1)}, bf16[256,128]{1,0:T(8,128)(2,1)}, u32[]{:S(2)}) copy-start(bf16[256,128]{1,0:T(8,128)(2,1)} %refs_2_.1) | copy-start | bytes 196612
  7.2 157.2 %all-gather.3.cloned.1.call-start = ((), (), s32[]{:S(2)}) async-start(), calls=%async_computation.3 | async-start | bytes 3022848 | tf_op jit(solution)/shard_map/all_gather | solution.py:841
  7.9 164.2 %all-gather.5.cloned.1.call-start = ((), (), s32[]{:S(2)}) async-start(), calls=%async_computation.4 | async-start | bytes 1511424 | tf_op jit(solution)/shard_map/all_gather | solution.py:842
  8.7 238.2 %reduce-scatter.12.cloned.1.call-start = ((), (), s32[]{:S(2)}) async-start(), calls=%async_computation.7 | async-start | bytes 1769472
  77.5 3.5 copy-start.5
  77.5 3.5 copy-start.10
  88.3 5.5 %copy-start.1 = (f32[1024,384]{1,0:T(8,128)}, f32[1024,384]{1,0:T(8,128)S(1)}, u32[]{:S(2)}) copy-start(f32[1024,384]{1,0:T(8,128)S(1)} %concatenate.13.cos_ref) | copy-start | bytes 4718596
  93.8 1.4 copy-start.3
  117.2 16.7 %copy-start.12 = (bf16[1024,768]{1,0:T(8,128)(2,1)}, bf16[1024,768]{1,0:T(8,128)(2,1)S(1)}, u32[]{:S(2)}) copy-start(bf16[1024,768]{1,0:T(8,128)(2,1)S(1)} %get-tuple-element.25.qkv_ref) | copy-start | bytes 4718596
  118.0 16.0 %copy-start.17 = (bf16[256,1024]{1,0:T(8,128)(2,1)S(1)}, bf16[256,1024]{1,0:T(8,128)(2,1)}, u32[]{:S(2)}) copy-start(bf16[256,1024]{1,0:T(8,128)(2,1)} %param.9) | copy-start | bytes 1572868
  133.9 1.2 copy-start.20
  134.0 1.4 copy-start
  134.1 1.0 copy-start.14
  161.6 1.3 copy-start.7
  163.0 1.4 copy-start.8
  172.1 9.0 %copy-start.9 = (bf16[1024,1024]{1,0:T(8,128)(2,1)S(1)}, bf16[1024,1024]{1,0:T(8,128)(2,1)}, u32[]{:S(2)}) copy-start(bf16[1024,1024]{1,0:T(8,128)(2,1)} %copy-done.8) | copy-start | bytes 6291460
  180.0 1.1 copy-start.22
  184.3 95.6 %reduce-scatter.8.cloned.1.call-start = ((), (), s32[]{:S(2)}) async-start(), calls=%async_computation.5 | async-start | bytes 2621440 | tf_op jit(solution)/shard_map/reduce_scatter | solution.py:870
  189.2 1.3 copy-start.23
  189.3 200.8 %reduce-scatter.10.cloned.1.call-start = ((), (), s32[]{:S(2)}) async-start(), calls=%async_computation.6 | async-start | bytes 3244032
  208.1 15.8 %copy-start.15 = (f32[256,1024]{1,0:T(8,128)S(1)}, f32[256,1024]{1,0:T(8,128)}, u32[]{:S(2)}) copy-start(f32[256,1024]{1,0:T(8,128)} %copy-done.14) | copy-start | bytes 3145732
  297.6 1.4 copy-start.2
  297.7 1.9 copy-start.13
  325.0 1.4 copy-start.11
  326.4 1.8 copy-start.6
  330.2 44.7 %copy-start.18 = (bf16[256,1024]{1,0:T(8,128)(2,1)S(1)}, bf16[256,1024]{1,0:T(8,128)(2,1)}, u32[]{:S(2)}) copy-start(bf16[256,1024]{1,0:T(8,128)(2,1)} %param.9) | copy-start | bytes 1572868
  330.2 44.7 %copy-start.21 = (f32[1024]{0:T(1024)S(1)}, f32[1024]{0:T(1024)}, u32[]{:S(2)}) copy-start(f32[1024]{0:T(1024)} %param.10) | copy-start | bytes 12292
  374.9 13.9 %copy-start.19 = (f32[256,1024]{1,0:T(8,128)S(1)}, f32[256,1024]{1,0:T(8,128)}, u32[]{:S(2)}) copy-start(f32[256,1024]{1,0:T(8,128)} %get-tuple-element.47) | copy-start | bytes 3145732
Sparse Core Ops, SparseCore 0:
  10.1 79.2 all-gather.2
  91.4 42.7 all-gather.4
  184.4 62.5 reduce-scatter.11
  249.5 30.3 reduce-scatter.7
  283.2 87.4 reduce-scatter.9

commit v2 on v1

--- a/solution.py
+++ b/solution.py
@@ -44,67 +44,81 @@
     return jnp.where(lane < 32, pltpu.roll(wide, width - 32, 1), pltpu.roll(wide, 32, 1))
 
 
+def wide_tables(cos_ref, sin_ref):
+    cos_two, sin_two = cos_ref[...], sin_ref[...]
+    ones, zeros = jnp.ones_like(cos_two), jnp.zeros_like(sin_two)
+    return (
+        jnp.concatenate([cos_two, cos_two, ones] * 2, axis=1),
+        jnp.concatenate([sin_two, sin_two, zeros] * 2, axis=1),
+    )
+
+
 def attend_kernel(mixed_ref, cos_ref, sin_ref, segc_ref, segr_ref, qkv_ref, att_ref, lse_ref):
     mixed = mixed_ref[...]
-    qkv_ref[...] = (mixed * cos_ref[...] + swap_halves(mixed) * sin_ref[...]).astype(BF)
+    cos_wide, sin_wide = wide_tables(cos_ref, sin_ref)
+    qkv_ref[...] = (mixed * cos_wide + swap_halves(mixed) * sin_wide).astype(BF)
     rows = mixed_ref.shape[0]
     block = 256
-    for head in range(2):
-        base = head * 192
-        keys = qkv_ref[:, base + 64 : base + 128]
-        values_t = qkv_ref[:, base + 128 : base + 192].astype(F32).T.astype(BF)
-
-        def step(i, carry):
-            start = pl.multiple_of(i * block, block)
+    values_t = [
+        qkv_ref[:, h * 192 + 128 : h * 192 + 192].astype(F32).T.astype(BF) for h in range(2)
+    ]
+
+    def step(i, carry):
+        start = pl.multiple_of(i * block, block)
+        same = segc_ref[...] == segr_ref[:, pl.ds(start, block)]
+        for head in range(2):
+            base = head * 192
             query = qkv_ref[pl.ds(start, block), base : base + 64] * BF(0.125)
-            scores = dot_last(keys, query)
-            same = segc_ref[...] == segr_ref[:, pl.ds(start, block)]
+            scores = dot_last(qkv_ref[:, base + 64 : base + 128], query)
             scores = jnp.where(same, scores, MASKED_SCORE)
             top = jnp.max(scores, axis=0, keepdims=True)
             expo = jnp.exp(scores - top)
             total = jnp.sum(expo, axis=0, keepdims=True)
             weights = (expo * (1.0 / total)).astype(BF)
-            out_t = dot_plain(values_t, weights)
+            out_t = dot_plain(values_t[head], weights)
             att_ref[pl.ds(start, block), head * 64 : head * 64 + 64] = out_t.T.astype(BF)
             lse_ref[0, head : head + 1, pl.ds(start, block)] = top + jnp.log(total)
-            return carry
-
-        lax.fori_loop(0, rows // block, step, 0)
+        return carry
+
+    lax.fori_loop(0, rows // block, step, 0)
 
 
 def attend_back_kernel(qkv_ref, ga_ref, lse_ref, cos_ref, sin_ref, segc_ref, segr_ref, gm_ref, acc):
     rows = qkv_ref.shape[0]
     block = 256
+    keys_t = [
+        qkv_ref[:, h * 192 + 64 : h * 192 + 128].astype(F32).T.astype(BF) for h in range(2)
+    ]
+
+    def step(i, carry):
+        start = pl.multiple_of(i * block, block)
+        same = segc_ref[...] == segr_ref[:, pl.ds(start, block)]
+        sums = []
+        for head in range(2):
+            base = head * 192
+            query = qkv_ref[pl.ds(start, block), base : base + 64] * BF(0.125)
+            grad_o = ga_ref[pl.ds(start, block), head * 64 : head * 64 + 64]
+            scores = dot_last(qkv_ref[:, base + 64 : base + 128], query)
+            scores = jnp.where(same, scores, MASKED_SCORE)
+            probs = jnp.exp(scores - lse_ref[0, head : head + 1, pl.ds(start, block)])
+            grad_p = dot_last(qkv_ref[:, base + 128 : base + 192], grad_o)
+            inner = jnp.sum(probs * grad_p, axis=0, keepdims=True)
+            grad_s = (probs * (grad_p - inner)).astype(BF)
+            sums.append(carry[2 * head] + dot_plain(grad_s, query))
+            sums.append(carry[2 * head + 1] + dot_plain(probs.astype(BF), grad_o))
+            grad_q = dot_plain(keys_t[head], grad_s) * 0.125
+            acc[pl.ds(start, block), base : base + 64] = grad_q.T
+        return tuple(sums)
+
+    empty = jnp.zeros((rows, 64), F32)
+    sums = lax.fori_loop(0, rows // block, step, (empty,) * 4)
     for head in range(2):
         base = head * 192
-        keys = qkv_ref[:, base + 64 : base + 128]
-        keys_t = keys.astype(F32).T.astype(BF)
-        values = qkv_ref[:, base + 128 : base + 192]
-
-        def step(i, carry):
-            grad_k, grad_v = carry
-            start = pl.multiple_of(i * block, block)
-            query = qkv_ref[pl.ds(start, block), base : base + 64] * BF(0.125)
-            grad_o = ga_ref[pl.ds(start, block), head * 64 : head * 64 + 64]
-            scores = dot_last(keys, query)
-            same = segc_ref[...] == segr_ref[:, pl.ds(start, block)]
-            scores = jnp.where(same, scores, MASKED_SCORE)
-            probs = jnp.exp(scores - lse_ref[0, head : head + 1, pl.ds(start, block)])
-            grad_p = dot_last(values, grad_o)
-            inner = jnp.sum(probs * grad_p, axis=0, keepdims=True)
-            grad_s = (probs * (grad_p - inner)).astype(BF)
-            grad_v = grad_v + dot_plain(probs.astype(BF), grad_o)
-            grad_k = grad_k + dot_plain(grad_s, query)
-            grad_q = dot_plain(keys_t, grad_s) * 0.125
-            acc[pl.ds(start, block), base : base + 64] = grad_q.T
-            return grad_k, grad_v
-
-        empty = jnp.zeros((rows, 64), F32)
-        grad_k, grad_v = lax.fori_loop(0, rows // block, step, (empty, empty))
-        acc[:, base + 64 : base + 128] = grad_k
-        acc[:, base + 128 : base + 192] = grad_v
+        acc[:, base + 64 : base + 128] = sums[2 * head]
+        acc[:, base + 128 : base + 192] = sums[2 * head + 1]
     grads = acc[...]
-    gm_ref[...] = (grads * cos_ref[...] - swap_halves(grads) * sin_ref[...]).astype(BF)
+    cos_wide, sin_wide = wide_tables(cos_ref, sin_ref)
+    gm_ref[...] = (grads * cos_wide - swap_halves(grads) * sin_wide).astype(BF)
 
 
 def attend(mixed, cos_wide, sin_wide, seg_col, seg_row):
@@ -116,8 +130,8 @@
         grid=(pairs,),
         in_specs=[
             pl.BlockSpec((rows, 384), lambda p: (0, p)),
-            pl.BlockSpec((rows, 384), whole),
-            pl.BlockSpec((rows, 384), whole),
+            pl.BlockSpec((rows, 64), whole),
+            pl.BlockSpec((rows, 64), whole),
             pl.BlockSpec((rows, 1), whole),
             pl.BlockSpec((1, rows), whole),
         ],
@@ -152,8 +166,8 @@
             pl.BlockSpec((rows, 384), lambda p: (0, p)),
             pl.BlockSpec((rows, 128), lambda p: (0, p)),
             pl.BlockSpec((1, 2, rows), lambda p: (p, 0, 0)),
-            pl.BlockSpec((rows, 384), whole),
-            pl.BlockSpec((rows, 384), whole),
+            pl.BlockSpec((rows, 64), whole),
+            pl.BlockSpec((rows, 64), whole),
             pl.BlockSpec((rows, 1), whole),
             pl.BlockSpec((1, rows), whole),
         ],
@@ -447,50 +461,42 @@
     )(*args)
 
 
-def gather_rows(ident, *arrays):
-    count = len(arrays)
-    per = len(RowGather.sems)
-
-    def kernel(*refs):
-        sems = refs[2 * count :]
-        run_parts(
-            [RowGather(refs[i], refs[count + i], sems[i * per : (i + 1) * per]) for i in range(count)], []
-        )
-
-    return comm_call(
-        kernel, arrays, [((4 * a.shape[0], a.shape[1]), BF) for a in arrays],
-        [pl.ANY] * count, RowGather.sems * count, ident, "gather_rows")
-
-
-def gather_first(ident, rows, weights, axes):
-    count = 1 + len(weights)
+def gather_parts(ident, rows, weights=(), axes=()):
+    near_count, count = len(rows), len(rows) + len(weights)
     per_row, per_weight = len(RowGather.sems), len(WeightGather.sems)
 
     def kernel(*refs):
         ins, outs, sems = refs[:count], refs[count : 2 * count], refs[2 * count :]
-        near = [RowGather(ins[0], outs[0], sems[:per_row])]
-        sems = sems[per_row:]
+        near = [
+            RowGather(ins[i], outs[i], sems[i * per_row : (i + 1) * per_row])
+            for i in range(near_count)
+        ]
+        sems = sems[near_count * per_row :]
         far = [
-            WeightGather(ins[1 + i], outs[1 + i], sems[i * per_weight : (i + 1) * per_weight], axes[i])
+            WeightGather(
+                ins[near_count + i], outs[near_count + i],
+                sems[i * per_weight : (i + 1) * per_weight], axes[i])
             for i in range(len(weights))
         ]
         run_parts(near, far)
 
-    shapes = [((4 * rows.shape[0], rows.shape[1]), BF)]
+    shapes = [((4 * a.shape[0], a.shape[1]), BF) for a in rows]
     for weight, axis in zip(weights, axes):
         shape = list(weight.shape)
         shape[axis] = shape[axis] * 8
         shapes.append((tuple(shape), BF))
     return comm_call(
-        kernel, (rows, *weights), shapes, [pl.ANY] * count,
-        RowGather.sems + WeightGather.sems * len(weights), ident, "gather_first")
-
-
-def reduce_sums(ident, partial, grads, axes):
-    rows = partial.shape[0] // 4
-    count = 1 + len(grads)
-    shapes = [((rows, partial.shape[1]), F32)]
-    scratch = RowReduce.scratch(rows, partial.shape[1]) + RowReduce.sems
+        kernel, (*rows, *weights), shapes, [pl.ANY] * count,
+        RowGather.sems * near_count + WeightGather.sems * len(weights), ident, "gather_parts")
+
+
+def reduce_sums(ident, partials, grads=(), axes=()):
+    near_count, count = len(partials), len(partials) + len(grads)
+    shapes, scratch = [], []
+    for partial in partials:
+        shape = (partial.shape[0] // 4, partial.shape[1])
+        shapes.append((shape, F32))
+        scratch = scratch + RowReduce.scratch(*shape) + RowReduce.sems
     for grad, axis in zip(grads, axes):
         shape = list(grad.shape)
         shape[axis] = shape[axis] // 8
@@ -499,14 +505,17 @@
 
     def kernel(*refs):
         ins, outs, rest = refs[:count], refs[count : 2 * count], refs[2 * count :]
-        near = [RowReduce(ins[0], outs[0], rest[:4], rest[4:8])]
+        near = []
+        for i in range(near_count):
+            near.append(RowReduce(ins[i], outs[i], rest[:4], rest[4:8]))
+            rest = rest[8:]
         far = []
         for i in range(len(grads)):
-            mine = rest[8 + 5 * i : 13 + 5 * i]
-            far.append(WeightReduce(ins[1 + i], outs[1 + i], mine[:3], mine[3:], axes[i]))
+            far.append(WeightReduce(ins[near_count + i], outs[near_count + i], rest[:3], rest[3:5], axes[i]))
+            rest = rest[5:]
         run_parts(near, far)
 
-    return comm_call(kernel, (partial, *grads), shapes, [VM] * count, scratch, ident, "reduce_sums")
+    return comm_call(kernel, (*partials, *grads), shapes, [VM] * count, scratch, ident, "reduce_sums")
 
 
 def sum_gains_kernel(part_ref, out_ref, near_in, mid, far_in, send_n, recv_n, send_f, recv_f):
@@ -838,26 +847,25 @@
     hidden_local = in_weight.shape[2]
     row_data = tokens.astype(F32)
     normed_attn, unit_attn, inverse_attn = layer_norm(row_data, attn_gain)
-    in_full = lax.all_gather(in_weight, "dp", axis=0, tiled=True)
-    down_full = lax.all_gather(down_weight, "dp", axis=1, tiled=True)
-    attn_input, qkv_flat, out_full = gather_first(
+    attn_input, cotangent_rows, qkv_flat, out_full = gather_parts(
         1,
-        normed_attn.astype(BF),
+        (normed_attn.astype(BF), cotangent),
         (qkv_weight.reshape(qkv_weight.shape[0], heads_local * 3 * head_dim), out_weight),
         (0, 1),
     )
+    in_shard = in_weight.reshape(in_weight.shape[0], 2 * hidden_local)
+    in_shard, attn_input = lax.optimization_barrier((in_shard, attn_input))
+    in_flat = lax.all_gather(in_shard, "dp", axis=0, tiled=True)
     seg_ids, position = segment_info(seg_lengths[0], pack_rows)
     cos_table, sin_table = rotary(position, head_dim)
-    ones, zeros = jnp.ones((pack_rows, head_dim), F32), jnp.zeros((pack_rows, head_dim), F32)
-    cos_wide = jnp.concatenate([cos_table] * 4 + [ones] + [cos_table] * 4 + [ones], axis=1)
-    sin_wide = jnp.concatenate(([-sin_table, sin_table] * 2 + [zeros]) * 2, axis=1)
+    cos_two = jnp.concatenate([cos_table, cos_table], axis=1)
+    sin_two = jnp.concatenate([-sin_table, sin_table], axis=1)
     seg_col, seg_row = seg_ids[:, None], seg_ids[None, :]
     mixed_proj = dot_plain(attn_input, qkv_flat)
-    qkv_rows, attended, log_totals = attend(mixed_proj, cos_wide, sin_wide, seg_col, seg_row)
-    residual = row_data + reduce_sums(2, dot_plain(attended, out_full).astype(BF), (), ())[0]
+    qkv_rows, attended, log_totals = attend(mixed_proj, cos_two, sin_two, seg_col, seg_row)
+    residual = row_data + reduce_sums(2, (dot_plain(attended, out_full).astype(BF),))[0]
     normed_mlp, unit_mlp, inverse_mlp = layer_norm(residual, mlp_gain)
-    mlp_rows, cotangent_rows = gather_rows(3, normed_mlp.astype(BF), cotangent)
-    in_flat = in_full.reshape(model_width, -1)
+    mlp_rows, down_full = gather_parts(3, (normed_mlp.astype(BF),), (down_weight,), (1,))
     lifted = dot_plain(mlp_rows, in_flat)
     gate = lifted[:, hidden_local:]
     act_gelu, act_slope = gelu_parts(lifted[:, :hidden_local])
@@ -866,34 +874,37 @@
     grad_lifted = jnp.concatenate(
         [grad_act * gate * act_slope, grad_act * act_gelu], axis=1
     ).astype(BF)
-    grad_mlp_in = reduce_sums(4, dot_last(grad_lifted, in_flat).astype(BF), (), ())[0]
-    layer_sum = lax.psum_scatter(
-        dot_plain(activated, down_full).astype(BF), "tensor", scatter_dimension=0, tiled=True
-    )
-    layer_out = (residual + layer_sum.astype(F32)).astype(BF)
-    grad_in_part = dot_first(mlp_rows, grad_lifted).reshape(in_full.shape)
-    grad_down_part = dot_first(activated, cotangent_rows)
     in_grad = lax.psum_scatter(
-        grad_in_part.astype(BF), "dp", scatter_dimension=0, tiled=True
-    ).astype(F32)
-    down_grad = lax.psum_scatter(
-        grad_down_part.astype(BF), "dp", scatter_dimension=1, tiled=True
-    ).astype(F32)
+        dot_first(mlp_rows, grad_lifted).astype(BF), "dp", scatter_dimension=0, tiled=True
+    )
+    in_grad = in_grad.reshape(in_weight.shape).astype(F32)
+    grad_mlp_in, down_grad = reduce_sums(
+        4,
+        (dot_last(grad_lifted, in_flat).astype(BF),),
+        (dot_first(activated, cotangent_rows).astype(BF),),
+        (1,),
+    )
+    layer_part = dot_plain(activated, down_full).astype(BF)
     grad_resid_norm, mlp_gain_part = norm_back(grad_mlp_in, unit_mlp, inverse_mlp, mlp_gain)
     grad_residual = cotangent.astype(F32) + grad_resid_norm
-    grad_branch = gather_rows(5, grad_residual.astype(BF))[0]
+    grad_branch = gather_parts(5, (grad_residual.astype(BF),))[0]
     grad_out_part = dot_first(attended, grad_branch).astype(BF)
     grad_attended = dot_last(grad_branch, out_full).astype(BF)
     grad_mixed = attend_back(
-        qkv_rows, grad_attended, log_totals, cos_wide, sin_wide, seg_col, seg_row
+        qkv_rows, grad_attended, log_totals, cos_two, sin_two, seg_col, seg_row
     )
     grad_qkv_part = dot_first(attn_input, grad_mixed).astype(BF)
-    grad_attn_in, qkv_grad, out_grad = reduce_sums(
-        6, dot_last(grad_mixed, qkv_flat).astype(BF), (grad_qkv_part, grad_out_part), (0, 1)
-    )
+    grad_attn_in, layer_sum, qkv_grad, out_grad = reduce_sums(
+        6,
+        (dot_last(grad_mixed, qkv_flat).astype(BF), layer_part),
+        (grad_qkv_part, grad_out_part),
+        (0, 1),
+    )
+    layer_out = (residual + layer_sum).astype(BF)
     grad_rows_attn, attn_gain_part = norm_back(grad_attn_in, unit_attn, inverse_attn, attn_gain)
     grad_tokens = (grad_residual + grad_rows_attn).astype(BF)
-    gains = sum_gains(7, jnp.concatenate([attn_gain_part[None], mlp_gain_part[None], jnp.zeros((6, model_width), F32)]))
+    gains = sum_gains(7, jnp.stack([attn_gain_part, mlp_gain_part]).reshape(8, model_width // 4))
+    gains = gains.reshape(2, model_width)
     return (
         layer_out,
         grad_tokens,

time: 407 us -> 331 us (0.81)
  waiting for transfers between devices: 55 us -> 0.04 us
  matrix products: 44.2 us -> 33.2 us
  local copies, waits for them, and re-layouts: 30.7 us -> 19.7 us
  Pallas kernels: 239 us -> 244 us
    reduce_scatter x1 -> x0, waiting for transfers between devices: 31.1 us -> none  [fast_body(): lax.psum_scatter(dot_plain(activated, down_full).astype(BF), 'tensor', sc...]
    unnamed x7 -> x3, waiting for transfers between devices: 23.9 us -> 0.03 us
    concatenate x3 -> x0, local copies, waits for them, and re-layouts: 8.7 us -> none  [the longest x1 5.42 us: fast_body(): jnp.concatenate(([-sin_table, sin_table] * 2 + [zeros]) * 2, axis=1)]
    pallas_call x7, Pallas kernels: 192 us -> 198 us  [comm_call(): pl.pallas_call(kernel, out_shape=[jax.ShapeDtypeStruct(*out) for out in o...]
    dot_general x4, matrix products: 16.6 us -> 11.6 us  [dot_last(): lax.dot_general(left, right, (((1,), (1,)), ((), ())), preferred_element_...]
    dot_general x4, matrix products: 16.8 us -> 11.9 us  [dot_plain(): return jnp.dot(left, right, preferred_element_type=jnp.float32)]
    unnamed x53 -> x77, local copies, waits for them, and re-layouts: 18.3 us -> 17.5 us
  transfers between devices with their start and end apart: 5 -> 2, of which waited for: 2 -> 0; matrix products, arithmetic and copies ran while one was open for 17% -> 9% of each run, Pallas kernels for 60% -> 62%
where the time goes in v2:
time: 331 us; the launch traced here: 326 us
  Pallas kernels  244 us (74%)
  matrix products  33.2 us (10%)
  local copies, waits for them, and re-layouts  19.7 us (6%)
  between operations  15.1 us (5%)
  other arithmetic  13.9 us (4%)
    pallas_call x7, Pallas kernels, comm_call(): pl.pallas_call(kernel, out_shape=[jax.ShapeDtypeStruct(*out) for out in o...  198 us
    pallas_call x1, Pallas kernels, attend_back(): pl.pallas_call(attend_back_kernel, grid=(pairs,), in_specs=[pl.BlockSpec(...  24.3 us
    pallas_call x1, Pallas kernels, attend(): pl.pallas_call(attend_kernel, grid=(pairs,), in_specs=[pl.BlockSpec((rows...  21.6 us
    unnamed x77, local copies, waits for them, and re-layouts  17.5 us
    dot_general x4, matrix products, dot_plain(): return jnp.dot(left, right, preferred_element_type=jnp.float32)  11.9 us
    dot_general x4, matrix products, dot_last(): lax.dot_general(left, right, (((1,), (1,)), ((), ())), preferred_element_...  11.6 us
    dot_general x4, matrix products, dot_first(): lax.dot_general(left, right, (((0,), (0,)), ((), ())), preferred_element_...  9.7 us
  transfers between devices with their start and end apart: 2, of which 0 were waited for; matrix products, arithmetic and copies ran while one was open for 9% of the time, Pallas kernels for 62%

profile of v2, /device:TPU:0, one launch (start us, length us, event | category | flops | bytes accessed | tf_op | source)
XLA Modules:
  0.0 326.0 jit_solution(8153183279376935625)
XLA Ops:
  7.2 0.0 all-gather.2.cloned.1.call-start
  7.2 1.2 convert_reduce_fusion
  8.5 1.3 fusion.18
  9.8 1.1 copy.31.refs_2_
  10.9 1.3 fusion.11.refs_0_
  12.3 41.7 %gather_parts.3 = (bf16[1024,1024]{1,0:T(8,128)(2,1)S(1)}, bf16[1024,1024]{1,0:T(8,128)(2,1)S(1)}, bf16[1024,768]{1,0:T(8,128)(2,1)S(1)}, bf16[256,1024]{1,0:T(8,128)(2,1)S(1)}) custom-call(bf16[256,1024]{1,0:T(8,128)(2,1)S(1)} %fusion.11.refs_0_, bf16[256,1024]{1,0:T(8,128)(2,1)S(1)} %copy-done, bf16[128,768]{1,0:T(8,128)(2,1)S(1)} %copy.31.refs_2_, ...), custom_call_target="tpu_custom_call" | custom-call | tf_op jit(solution)/shard_map/gather_parts/pallas_call | solution.py:451
  54.0 1.4 copy-done.9
  55.4 1.3 copy-done.12
  56.7 1.1 copy-done.16
  57.8 0.0 all-gather.2.cloned.1.call-update
  57.9 0.0 reduce-scatter.4.cloned.1.call-start
  57.9 0.2 reduce-window.8
  58.1 0.1 convert_reduce_fusion.1
  58.2 0.2 copy.33.segc_ref
  58.4 0.0 copy-start.1
  58.5 1.9 fusion.19
  60.4 0.3 pad_maximum_fusion.3
  60.8 3.4 %fusion.24.mixed_ref = f32[1024,768]{1,0:T(8,128)} fusion(bf16[1024,1024]{1,0:T(8,128)(2,1)S(1)} %copy-done.10, bf16[1024,768]{1,0:T(8,128)(2,1)S(1)} %copy-done.17), kind=kOutput, calls=%fused_computation.71 | convolution fusion | flops 1610612736 | bytes 6815744 | tf_op jit(solution)/shard_map/dot_general | solution.py:18
  64.2 21.6 %attend.1 = (bf16[1024,768]{1,0:T(8,128)(2,1)S(1)}, bf16[1024,256]{1,0:T(8,128)(2,1)S(1)}, f32[2,2,1024]{2,1,0:T(2,128)S(1)}) custom-call(f32[1024,768]{1,0:T(8,128)} %fusion.24.mixed_ref, f32[1024,64]{1,0:T(8,128)S(1)} %get-tuple-element.70.cos_ref, f32[1024,64]{1,0:T(8,128)S(1)} %get-tuple-element.71.sin_ref, s32[1024,1]{1,0:T(8,128)S(1)} %copy.33.segc_ref, ...), custom_call_target="tpu_custom_call" | custom-call | flops 1073741824 | bytes 6291456 | tf_op jit(solution)/shard_map/attend/pallas_call | solution.py:128
  85.8 0.7 convolution_convert_fusion.2.refs_0_
  86.5 16.1 %reduce_sums.3 = f32[256,1024]{1,0:T(8,128)S(1)} custom-call(bf16[1024,1024]{1,0:T(8,128)(2,1)S(1)} %convolution_convert_fusion.2.refs_0_), custom_call_target="tpu_custom_call" | custom-call | tf_op jit(solution)/shard_map/reduce_sums/pallas_call | solution.py:451
  102.7 0.0 copy-start.29
  102.7 0.0 copy-start.7
  102.7 0.2 fusion.23
  102.9 0.2 multiply_reduce_fusion.2
  103.1 0.7 copy-done.23
  103.9 0.2 multiply_convert_fusion.2.refs_0_
  104.1 32.3 %gather_parts.4 = (bf16[1024,1024]{1,0:T(8,128)(2,1)S(1)}, bf16[656,1024]{1,0:T(8,128)(2,1)S(1)}) custom-call(bf16[256,1024]{1,0:T(8,128)(2,1)S(1)} %multiply_convert_fusion.2.refs_0_, bf16[656,128]{1,0:T(8,128)(2,1)S(1)} %copy-done.7), custom_call_target="tpu_custom_call" | custom-call | tf_op jit(solution)/shard_map/gather_parts/pallas_call | solution.py:451
  136.4 1.3 copy-done.14
  137.8 5.9 %fusion.25 = f32[1024,1312]{0,1:T(8,128)S(1)} fusion(bf16[1024,1024]{1,0:T(8,128)(2,1)} %copy-done.14, bf16[1024,1312]{0,1:T(8,128)(2,1)} %all-gather.2.cloned.1.call-done), kind=kOutput, calls=%fused_computation.72 | convolution fusion | flops 2751463424 | bytes 10158080 | tf_op jit(solution)/shard_map/dot_general | solution.py:18
  143.7 3.0 fusion.4
  146.7 1.6 convolution_convert_fusion.6.refs_1_
  148.3 0.4 copy-done.34
  148.8 1.0 copy-done.15
  149.8 5.6 %convolution_convert_fusion = bf16[1024,1312]{0,1:T(8,128)(2,1)} fusion(bf16[1024,1024]{1,0:T(8,128)(2,1)S(1)} %copy-done.15, bf16[1024,656]{0,1:T(8,128)(2,1)S(1)} %get-tuple-element.63, bf16[1024,656]{0,1:T(8,128)(2,1)S(1)} %get-tuple-element.62), kind=kOutput, calls=%fused_computation.1 | convolution fusion | flops 2758180864 | bytes 7471104 | tf_op jit(solution)/shard_map/dot_general | solution.py:22
  155.3 4.5 %copy.36 = bf16[1024,1312]{1,0:T(8,128)(2,1)} copy(bf16[1024,1312]{0,1:T(8,128)(2,1)} %convolution_convert_fusion) | data formatting | bytes 5373952
  159.8 0.0 reduce-scatter.4.cloned.1.call-update
  159.9 6.1 %convolution_convert_fusion.1.refs_0_ = bf16[1024,1024]{1,0:T(8,128)(2,1)S(1)} fusion(bf16[1024,1312]{0,1:T(8,128)(2,1)} %all-gather.2.cloned.1.call-done, bf16[1024,656]{0,1:T(8,128)(2,1)} %copy-done.34, bf16[1024,656]{0,1:T(8,128)(2,1)} %copy-done.33), kind=kOutput, calls=%fused_computation.12 | convolution fusion | flops 2757885952 | bytes 7471104 | tf_op jit(solution)/shard_map/dot_general | solution.py:28
  165.9 37.0 %reduce_sums.4 = (f32[256,1024]{1,0:T(8,128)S(1)}, f32[656,128]{1,0:T(8,128)S(1)}) custom-call(bf16[1024,1024]{1,0:T(8,128)(2,1)S(1)} %convolution_convert_fusion.1.refs_0_, bf16[656,1024]{1,0:T(8,128)(2,1)S(1)} %convolution_convert_fusion.6.refs_1_), custom_call_target="tpu_custom_call" | custom-call | tf_op jit(solution)/shard_map/reduce_sums/pallas_call | solution.py:451
  202.9 0.5 multiply_reduce_fusion
  203.5 1.4 fusion.22
  204.9 15.8 %gather_parts.5 = bf16[1024,1024]{1,0:T(8,128)(2,1)S(1)} custom-call(bf16[256,1024]{1,0:T(8,128)(2,1)S(1)} %get-tuple-element.58.refs_0_), custom_call_target="tpu_custom_call" | custom-call | tf_op jit(solution)/shard_map/gather_parts/pallas_call | solution.py:451
  220.7 0.8 convolution_convert_fusion.8.ga_ref
  221.5 0.3 copy-done.2
  221.8 0.5 copy-done.22
  222.3 24.3 %attend_back.1 = bf16[1024,768]{1,0:T(8,128)(2,1)S(1)} custom-call(bf16[1024,768]{1,0:T(8,128)(2,1)S(1)} %copy-done.22, bf16[1024,256]{1,0:T(8,128)(2,1)S(1)} %convolution_convert_fusion.8.ga_ref, f32[2,2,1024]{2,1,0:T(2,128)S(1)} %get-tuple-element.36.lse_ref, f32[1024,64]{1,0:T(8,128)S(1)} %get-tuple-element.70.cos_ref, ...), custom_call_target="tpu_custom_call" | custom-call | flops 2684354560 | bytes 6291456 | tf_op jit(solution)/shard_map/attend_back/pallas_call | solution.py:162
  246.6 0.7 convolution_convert_fusion.7.refs_3_
  247.4 0.6 copy-done.20
  248.0 0.4 copy-done.32
  248.4 1.8 convolution_convert_fusion.3.refs_1_
  250.3 1.8 convolution_convert_fusion.4.refs_0_
  252.1 1.9 convolution_convert_fusion.5.refs_2_
  254.0 44.4 %reduce_sums.5 = (f32[256,1024]{1,0:T(8,128)S(1)}, f32[256,1024]{1,0:T(8,128)S(1)}, f32[128,768]{1,0:T(8,128)S(1)}, f32[256,128]{1,0:T(8,128)S(1)}) custom-call(bf16[1024,1024]{1,0:T(8,128)(2,1)S(1)} %convolution_convert_fusion.4.refs_0_, bf16[1024,1024]{1,0:T(8,128)(2,1)S(1)} %convolution_convert_fusion.3.refs_1_, ...), custom_call_target="tpu_custom_call" | custom-call | tf_op jit(solution)/shard_map/reduce_sums/pallas_call | solution.py:451
  298.4 0.5 fusion.17
  299.0 10.7 %sum_gains.1 = f32[8,256]{1,0:T(8,128)S(1)} custom-call(f32[8,256]{1,0:T(8,128)S(1)} %reshape.118.part_ref), custom_call_target="tpu_custom_call" | custom-call | tf_op jit(solution)/shard_map/sum_gains/pallas_call | solution.py:451
  309.7 0.6 copy.39
  310.3 0.6 copy.38
  310.9 0.9 copy.35
  311.8 2.2 add_convert_fusion
  314.0 1.2 fusion.16
  315.2 1.2 copy.37
  316.4 0.9 convert.9
  317.3 0.7 copy.42
  318.0 0.7 copy.43
  (71 shorter events, 0.2 us)
Async XLA Ops:
  7.2 5.1 %copy-start = (bf16[256,1024]{1,0:T(8,128)(2,1)S(1)}, bf16[256,1024]{1,0:T(8,128)(2,1)}, u32[]{:S(2)}) copy-start(bf16[256,1024]{1,0:T(8,128)(2,1)} %refs_1_.2) | copy-start | bytes 1572868
  7.2 5.1 %copy-start.8 = (bf16[256,128]{1,0:T(8,128)(2,1)S(1)}, bf16[256,128]{1,0:T(8,128)(2,1)}, u32[]{:S(2)}) copy-start(bf16[256,128]{1,0:T(8,128)(2,1)} %refs_3_.1) | copy-start | bytes 196612
  7.2 50.7 %copy-start.30 = (s32[1,3]{1,0:T(1,128)S(1)}, s32[1,3]{1,0:T(1,128)}, u32[]{:S(2)}) copy-start(s32[1,3]{1,0:T(1,128)} %param.16) | copy-start | bytes 40
  7.2 130.6 %all-gather.2.cloned.1.call-start = ((), (), s32[]{:S(2)}) async-start(), calls=%async_computation.1 | async-start | bytes 3022848 | tf_op jit(solution)/shard_map/all_gather | solution.py:858
  54.0 1.4 copy-start.9
  55.4 1.3 copy-start.12
  56.7 1.1 copy-start.16
  57.8 27.9 %copy-start.3 = (bf16[256,1024]{1,0:T(8,128)(2,1)}, bf16[256,1024]{1,0:T(8,128)(2,1)S(1)}, u32[]{:S(2)}) copy-start(bf16[256,1024]{1,0:T(8,128)(2,1)S(1)} %get-tuple-element.29) | copy-start | bytes 1572868
  57.9 257.4 %reduce-scatter.4.cloned.1.call-start = ((), (), s32[]{:S(2)}) async-start(), calls=%async_computation.2 | async-start | bytes 3244032
  58.4 5.8 %copy-start.1 = (s32[1024,1]{1,0:T(8,128)}, s32[1024,1]{1,0:T(8,128)S(1)}, u32[]{:S(2)}) copy-start(s32[1024,1]{1,0:T(8,128)S(1)} %copy.33.segc_ref) | copy-start | bytes 12292
  58.5 2.3 copy-start.10
  58.5 2.3 copy-start.17
  85.8 16.9 %copy-start.21 = (bf16[1024,768]{1,0:T(8,128)(2,1)}, bf16[1024,768]{1,0:T(8,128)(2,1)S(1)}, u32[]{:S(2)}) copy-start(bf16[1024,768]{1,0:T(8,128)(2,1)S(1)} %get-tuple-element.30.qkv_ref) | copy-start | bytes 4718596
  86.5 16.1 %copy-start.25 = (bf16[256,1024]{1,0:T(8,128)(2,1)S(1)}, bf16[256,1024]{1,0:T(8,128)(2,1)}, u32[]{:S(2)}) copy-start(bf16[256,1024]{1,0:T(8,128)(2,1)} %param.9) | copy-start | bytes 1572868
  102.7 1.2 copy-start.29
  102.7 1.4 copy-start.7
  102.9 1.0 copy-start.23
  136.4 1.3 copy-start.14
  137.8 5.9 %copy-start.19 = (bf16[656,1024]{1,0:T(8,128)(2,1)}, bf16[656,1024]{1,0:T(8,128)(2,1)S(1)}, u32[]{:S(2)}) copy-start(bf16[656,1024]{1,0:T(8,128)(2,1)S(1)} %get-tuple-element.32) | copy-start | bytes 4030468
  137.8 5.9 %copy-start.13 = (bf16[1024,1024]{1,0:T(8,128)(2,1)S(1)}, bf16[1024,1024]{1,0:T(8,128)(2,1)}, u32[]{:S(2)}) copy-start(bf16[1024,1024]{1,0:T(8,128)(2,1)} %copy-done.12) | copy-start | bytes 6291460
  146.7 1.6 copy-start.31
  146.7 1.6 copy-start.33
  146.7 2.0 copy-start.34
  146.7 3.0 copy-start.15
  165.9 37.0 %copy-start.24 = (f32[256,1024]{1,0:T(8,128)S(1)}, f32[256,1024]{1,0:T(8,128)}, u32[]{:S(2)}) copy-start(f32[256,1024]{1,0:T(8,128)} %copy-done.23) | copy-start | bytes 3145732
  202.9 2.0 copy-start.5
  204.9 15.8 %copy-start.4 = (bf16[256,1024]{1,0:T(8,128)(2,1)S(1)}, bf16[256,1024]{1,0:T(8,128)(2,1)}, u32[]{:S(2)}) copy-start(bf16[256,1024]{1,0:T(8,128)(2,1)} %copy-done.3) | copy-start | bytes 1572868
  220.7 1.0 copy-start.2
  220.7 1.6 copy-start.22
  246.6 1.3 copy-start.20
  246.6 1.7 copy-start.32
  248.4 1.9 copy-start.18
  250.2 1.8 copy-start.11
  254.0 44.4 %copy-start.26 = (bf16[256,1024]{1,0:T(8,128)(2,1)S(1)}, bf16[256,1024]{1,0:T(8,128)(2,1)}, u32[]{:S(2)}) copy-start(bf16[256,1024]{1,0:T(8,128)(2,1)} %param.9) | copy-start | bytes 1572868
  254.0 44.4 %copy-start.28 = (f32[1024]{0:T(1024)S(1)}, f32[1024]{0:T(1024)}, u32[]{:S(2)}) copy-start(f32[1024]{0:T(1024)} %param.10) | copy-start | bytes 12292
  311.8 2.2 copy-start.27
  314.0 4.0 %copy-start.6 = (f32[656,128]{1,0:T(8,128)S(1)}, f32[656,128]{1,0:T(8,128)}, u32[]{:S(2)}) copy-start(f32[656,128]{1,0:T(8,128)} %copy-done.5) | copy-start | bytes 1007620
Sparse Core Ops, SparseCore 0:
  58.0 67.7 all-gather.1
  160.0 87.5 reduce-scatter.3

commit v3 on v2

--- a/solution.py
+++ b/solution.py
@@ -53,75 +53,114 @@
     )
 
 
-def attend_kernel(mixed_ref, cos_ref, sin_ref, segc_ref, segr_ref, qkv_ref, att_ref, lse_ref):
+BLOCK = 256
+
+
+def attend_kernel(
+    reach_ref, mixed_ref, cos_ref, sin_ref, segc_ref, segr_ref, qkv_ref, att_ref, lse_ref, values_t
+):
     mixed = mixed_ref[...]
     cos_wide, sin_wide = wide_tables(cos_ref, sin_ref)
     qkv_ref[...] = (mixed * cos_wide + swap_halves(mixed) * sin_wide).astype(BF)
     rows = mixed_ref.shape[0]
-    block = 256
-    values_t = [
-        qkv_ref[:, h * 192 + 128 : h * 192 + 192].astype(F32).T.astype(BF) for h in range(2)
-    ]
-
-    def step(i, carry):
-        start = pl.multiple_of(i * block, block)
-        same = segc_ref[...] == segr_ref[:, pl.ds(start, block)]
-        for head in range(2):
-            base = head * 192
-            query = qkv_ref[pl.ds(start, block), base : base + 64] * BF(0.125)
-            scores = dot_last(qkv_ref[:, base + 64 : base + 128], query)
-            scores = jnp.where(same, scores, MASKED_SCORE)
-            top = jnp.max(scores, axis=0, keepdims=True)
-            expo = jnp.exp(scores - top)
-            total = jnp.sum(expo, axis=0, keepdims=True)
-            weights = (expo * (1.0 / total)).astype(BF)
-            out_t = dot_plain(values_t[head], weights)
-            att_ref[pl.ds(start, block), head * 64 : head * 64 + 64] = out_t.T.astype(BF)
-            lse_ref[0, head : head + 1, pl.ds(start, block)] = top + jnp.log(total)
-        return carry
-
-    lax.fori_loop(0, rows // block, step, 0)
-
-
-def attend_back_kernel(qkv_ref, ga_ref, lse_ref, cos_ref, sin_ref, segc_ref, segr_ref, gm_ref, acc):
-    rows = qkv_ref.shape[0]
-    block = 256
-    keys_t = [
-        qkv_ref[:, h * 192 + 64 : h * 192 + 128].astype(F32).T.astype(BF) for h in range(2)
-    ]
-
-    def step(i, carry):
-        start = pl.multiple_of(i * block, block)
-        same = segc_ref[...] == segr_ref[:, pl.ds(start, block)]
-        sums = []
-        for head in range(2):
-            base = head * 192
-            query = qkv_ref[pl.ds(start, block), base : base + 64] * BF(0.125)
-            grad_o = ga_ref[pl.ds(start, block), head * 64 : head * 64 + 64]
-            scores = dot_last(qkv_ref[:, base + 64 : base + 128], query)
-            scores = jnp.where(same, scores, MASKED_SCORE)
-            probs = jnp.exp(scores - lse_ref[0, head : head + 1, pl.ds(start, block)])
-            grad_p = dot_last(qkv_ref[:, base + 128 : base + 192], grad_o)
-            inner = jnp.sum(probs * grad_p, axis=0, keepdims=True)
-            grad_s = (probs * (grad_p - inner)).astype(BF)
-            sums.append(carry[2 * head] + dot_plain(grad_s, query))
-            sums.append(carry[2 * head + 1] + dot_plain(probs.astype(BF), grad_o))
-            grad_q = dot_plain(keys_t[head], grad_s) * 0.125
-            acc[pl.ds(start, block), base : base + 64] = grad_q.T
-        return tuple(sums)
-
-    empty = jnp.zeros((rows, 64), F32)
-    sums = lax.fori_loop(0, rows // block, step, (empty,) * 4)
     for head in range(2):
         base = head * 192
-        acc[:, base + 64 : base + 128] = sums[2 * head]
-        acc[:, base + 128 : base + 192] = sums[2 * head + 1]
+        values_t[head] = qkv_ref[:, base + 128 : base + 192].astype(F32).T.astype(BF)
+
+    def step(i, carry):
+        window = pl.ds(pl.multiple_of(i * BLOCK, BLOCK), BLOCK)
+        queries = [qkv_ref[window, h * 192 : h * 192 + 64] * BF(0.125) for h in range(2)]
+        seg_query = segr_ref[:, window]
+
+        def inner(j, state):
+            near = pl.ds(pl.multiple_of(j * BLOCK, BLOCK), BLOCK)
+            same = segc_ref[near, :] == seg_query
+            after = []
+            for head in range(2):
+                top, total, out_t = state[3 * head : 3 * head + 3]
+                base = head * 192
+                scores = dot_last(qkv_ref[near, base + 64 : base + 128], queries[head])
+                scores = jnp.where(same, scores, MASKED_SCORE)
+                higher = jnp.maximum(top, jnp.max(scores, axis=0, keepdims=True))
+                scale = jnp.exp(top - higher)
+                expo = jnp.exp(scores - higher)
+                after.append(higher)
+                after.append(total * scale + jnp.sum(expo, axis=0, keepdims=True))
+                after.append(out_t * scale + dot_plain(values_t[head, :, near], expo.astype(BF)))
+            return tuple(after)
+
+        first = (
+            jnp.full((1, BLOCK), MASKED_SCORE, F32),
+            jnp.zeros((1, BLOCK), F32),
+            jnp.zeros((64, BLOCK), F32),
+        )
+        state = lax.fori_loop(reach_ref[0, i], reach_ref[1, i], inner, first * 2)
+        for head in range(2):
+            top, total, out_t = state[3 * head : 3 * head + 3]
+            out = (out_t * (1.0 / total)).T.astype(BF)
+            att_ref[window, head * 64 : head * 64 + 64] = out
+            lse_ref[0, head : head + 1, window] = top + jnp.log(total)
+        return carry
+
+    lax.fori_loop(0, rows // BLOCK, step, 0)
+
+
+def attend_back_kernel(
+    reach_ref, qkv_ref, ga_ref, att_ref, lse_ref, cos_ref, sin_ref, segc_ref, segr_ref,
+    gm_ref, acc, keys_t
+):
+    rows = qkv_ref.shape[0]
+    for head in range(2):
+        base = head * 192
+        keys_t[head] = qkv_ref[:, base + 64 : base + 128].astype(F32).T.astype(BF)
+    acc[...] = jnp.zeros_like(acc)
+
+    def step(i, carry):
+        window = pl.ds(pl.multiple_of(i * BLOCK, BLOCK), BLOCK)
+        queries = [qkv_ref[window, h * 192 : h * 192 + 64] * BF(0.125) for h in range(2)]
+        grads_o = [ga_ref[window, h * 64 : h * 64 + 64] for h in range(2)]
+        seg_query = segr_ref[:, window]
+        weighed = (ga_ref[window, :].astype(F32) * att_ref[window, :].astype(F32)).T
+        inners = [jnp.sum(weighed[h * 64 : h * 64 + 64], axis=0, keepdims=True) for h in range(2)]
+        totals = [lse_ref[0, h : h + 1, window] for h in range(2)]
+
+        def inner(j, grads_q):
+            near = pl.ds(pl.multiple_of(j * BLOCK, BLOCK), BLOCK)
+            same = segc_ref[near, :] == seg_query
+            after = []
+            for head in range(2):
+                base = head * 192
+                scores = dot_last(qkv_ref[near, base + 64 : base + 128], queries[head])
+                scores = jnp.where(same, scores, MASKED_SCORE)
+                probs = jnp.exp(scores - totals[head])
+                grad_p = dot_last(qkv_ref[near, base + 128 : base + 192], grads_o[head])
+                grad_s = (probs * (grad_p - inners[head])).astype(BF)
+                acc[near, base + 64 : base + 128] += dot_plain(grad_s, queries[head])
+                acc[near, base + 128 : base + 192] += dot_plain(probs.astype(BF), grads_o[head])
+                after.append(grads_q[head] + dot_plain(keys_t[head, :, near], grad_s))
+            return tuple(after)
+
+        empty = jnp.zeros((64, BLOCK), F32)
+        grads_q = lax.fori_loop(reach_ref[0, i], reach_ref[1, i], inner, (empty, empty))
+        for head in range(2):
+            acc[window, head * 192 : head * 192 + 64] = (grads_q[head] * 0.125).T
+        return carry
+
+    lax.fori_loop(0, rows // BLOCK, step, 0)
     grads = acc[...]
     cos_wide, sin_wide = wide_tables(cos_ref, sin_ref)
     gm_ref[...] = (grads * cos_wide - swap_halves(grads) * sin_wide).astype(BF)
 
 
-def attend(mixed, cos_wide, sin_wide, seg_col, seg_row):
+def block_reach(position):
+    starts = jnp.arange(position.shape[0] // BLOCK, dtype=jnp.int32) * BLOCK
+    low = (starts - position[::BLOCK]) // BLOCK
+    order = jnp.arange(low.shape[0], dtype=jnp.int32)
+    high = jnp.sum((low[None, :] <= order[:, None]).astype(jnp.int32), axis=1)
+    return jnp.stack([low, high])
+
+
+def attend(reach, mixed, cos_two, sin_two, seg_col, seg_row):
     rows, cols = mixed.shape
     pairs = cols // 384
     whole = lambda p: (0, 0)
@@ -129,6 +168,7 @@
         attend_kernel,
         grid=(pairs,),
         in_specs=[
+            pl.BlockSpec(memory_space=pltpu.SMEM),
             pl.BlockSpec((rows, 384), lambda p: (0, p)),
             pl.BlockSpec((rows, 64), whole),
             pl.BlockSpec((rows, 64), whole),
@@ -145,6 +185,7 @@
             jax.ShapeDtypeStruct((rows, pairs * 128), BF),
             jax.ShapeDtypeStruct((pairs, 2, rows), F32),
         ],
+        scratch_shapes=[VM((2, 64, rows), BF)],
         cost_estimate=pl.CostEstimate(
             flops=pairs * 2 * rows * rows * 64 * 4,
             transcendentals=pairs * 2 * rows * rows,
@@ -152,10 +193,10 @@
         ),
         compiler_params=pltpu.CompilerParams(vmem_limit_bytes=48 << 20),
         name="attend",
-    )(mixed, cos_wide, sin_wide, seg_col, seg_row)
-
-
-def attend_back(qkv, grad_att, lse, cos_wide, sin_wide, seg_col, seg_row):
+    )(reach, mixed, cos_two, sin_two, seg_col, seg_row)
+
+
+def attend_back(reach, qkv, grad_att, attended, lse, cos_two, sin_two, seg_col, seg_row):
     rows, cols = qkv.shape
     pairs = cols // 384
     whole = lambda p: (0, 0)
@@ -163,7 +204,9 @@
         attend_back_kernel,
         grid=(pairs,),
         in_specs=[
+            pl.BlockSpec(memory_space=pltpu.SMEM),
             pl.BlockSpec((rows, 384), lambda p: (0, p)),
+            pl.BlockSpec((rows, 128), lambda p: (0, p)),
             pl.BlockSpec((rows, 128), lambda p: (0, p)),
             pl.BlockSpec((1, 2, rows), lambda p: (p, 0, 0)),
             pl.BlockSpec((rows, 64), whole),
@@ -173,7 +216,7 @@
         ],
         out_specs=pl.BlockSpec((rows, 384), lambda p: (0, p)),
         out_shape=jax.ShapeDtypeStruct((rows, cols), BF),
-        scratch_shapes=[VM((rows, 384), F32)],
+        scratch_shapes=[VM((rows, 384), F32), VM((2, 64, rows), BF)],
         cost_estimate=pl.CostEstimate(
             flops=pairs * 2 * rows * rows * 64 * 10,
             transcendentals=pairs * 2 * rows * rows,
@@ -181,7 +224,7 @@
         ),
         compiler_params=pltpu.CompilerParams(vmem_limit_bytes=48 << 20),
         name="attend_back",
-    )(qkv, grad_att, lse, cos_wide, sin_wide, seg_col, seg_row)
+    )(reach, qkv, grad_att, attended, lse, cos_two, sin_two, seg_col, seg_row)
 
 
 def remote(source, target, send_sem, recv_sem, device):
@@ -861,8 +904,9 @@
     cos_two = jnp.concatenate([cos_table, cos_table], axis=1)
     sin_two = jnp.concatenate([-sin_table, sin_table], axis=1)
     seg_col, seg_row = seg_ids[:, None], seg_ids[None, :]
+    reach = block_reach(position)
     mixed_proj = dot_plain(attn_input, qkv_flat)
-    qkv_rows, attended, log_totals = attend(mixed_proj, cos_two, sin_two, seg_col, seg_row)
+    qkv_rows, attended, log_totals = attend(reach, mixed_proj, cos_two, sin_two, seg_col, seg_row)
     residual = row_data + reduce_sums(2, (dot_plain(attended, out_full).astype(BF),))[0]
     normed_mlp, unit_mlp, inverse_mlp = layer_norm(residual, mlp_gain)
     mlp_rows, down_full = gather_parts(3, (normed_mlp.astype(BF),), (down_weight,), (1,))
@@ -891,7 +935,7 @@
     grad_out_part = dot_first(attended, grad_branch).astype(BF)
     grad_attended = dot_last(grad_branch, out_full).astype(BF)
     grad_mixed = attend_back(
-        qkv_rows, grad_attended, log_totals, cos_two, sin_two, seg_col, seg_row
+        reach, qkv_rows, grad_attended, attended, log_totals, cos_two, sin_two, seg_col, seg_row
     )
     grad_qkv_part = dot_first(attn_input, grad_mixed).astype(BF)
     grad_attn_in, layer_sum, qkv_grad, out_grad = reduce_sums(

time: 331 us -> 325 us (0.982); the launches traced: 326 us -> 324 us
    pallas_call x7, Pallas kernels: 198 us -> 205 us  [comm_call(): pl.pallas_call(kernel, out_shape=[jax.ShapeDtypeStruct(*out) for out in o...]
    pallas_call x1, Pallas kernels: 24.3 us -> 18.5 us  [attend_back(): pl.pallas_call(attend_back_kernel, grid=(pairs,), in_specs=[pl.BlockSpec(...]
where the time goes in v3:
time: 325 us; the launch traced here: 324 us
  Pallas kernels  242 us (74%)
  matrix products  33.2 us (10%)
  local copies, waits for them, and re-layouts  19.8 us (6%)
  between operations  14.7 us (5%)
  other arithmetic  14.2 us (4%)
    pallas_call x7, Pallas kernels, comm_call(): pl.pallas_call(kernel, out_shape=[jax.ShapeDtypeStruct(*out) for out in o...  205 us
    pallas_call x1, Pallas kernels, attend(): pl.pallas_call(attend_kernel, grid=(pairs,), in_specs=[pl.BlockSpec(memor...  19.1 us
    pallas_call x1, Pallas kernels, attend_back(): pl.pallas_call(attend_back_kernel, grid=(pairs,), in_specs=[pl.BlockSpec(...  18.5 us
    unnamed x77, local copies, waits for them, and re-layouts  17.5 us
    dot_general x4, matrix products, dot_plain(): return jnp.dot(left, right, preferred_element_type=jnp.float32)  11.9 us
    dot_general x4, matrix products, dot_last(): lax.dot_general(left, right, (((1,), (1,)), ((), ())), preferred_element_...  11.6 us
    dot_general x4, matrix products, dot_first(): lax.dot_general(left, right, (((0,), (0,)), ((), ())), preferred_element_...  9.6 us
  transfers between devices with their start and end apart: 2, of which 0 were waited for; matrix products, arithmetic and copies ran while one was open for 9% of the time, Pallas kernels for 62%

profile of v3, /device:TPU:0, one launch (start us, length us, event | category | flops | bytes accessed | tf_op | source)
XLA Modules:
  0.0 324.1 jit_solution(2630412632331473223)
XLA Ops:
  7.2 0.0 all-gather.2.cloned.1.call-start
  7.2 1.2 convert_reduce_fusion
  8.5 1.3 fusion.18
  9.8 1.1 copy.31.refs_2_
  10.9 1.3 fusion.11.refs_0_
  12.3 41.7 %gather_parts.3 = (bf16[1024,1024]{1,0:T(8,128)(2,1)S(1)}, bf16[1024,1024]{1,0:T(8,128)(2,1)S(1)}, bf16[1024,768]{1,0:T(8,128)(2,1)S(1)}, bf16[256,1024]{1,0:T(8,128)(2,1)S(1)}) custom-call(bf16[256,1024]{1,0:T(8,128)(2,1)S(1)} %fusion.11.refs_0_, bf16[256,1024]{1,0:T(8,128)(2,1)S(1)} %copy-done, bf16[128,768]{1,0:T(8,128)(2,1)S(1)} %copy.31.refs_2_, ...), custom_call_target="tpu_custom_call" | custom-call | tf_op jit(solution)/shard_map/gather_parts/pallas_call | solution.py:494
  54.0 1.4 copy-done.9
  55.4 1.3 copy-done.12
  56.7 1.1 copy-done.16
  57.8 0.0 all-gather.2.cloned.1.call-update
  57.9 0.0 reduce-scatter.4.cloned.1.call-start
  57.9 0.2 reduce-window.8
  58.1 0.1 convert_reduce_fusion.1
  58.2 0.1 slice.17
  58.3 0.2 copy.33.segc_ref
  58.6 0.1 convert_reduce_fusion.2
  58.7 1.9 fusion.19
  60.7 0.3 pad_maximum_fusion.3
  61.0 3.4 %fusion.25.mixed_ref = f32[1024,768]{1,0:T(8,128)} fusion(bf16[1024,1024]{1,0:T(8,128)(2,1)S(1)} %copy-done.10, bf16[1024,768]{1,0:T(8,128)(2,1)S(1)} %copy-done.17), kind=kOutput, calls=%fused_computation.79 | convolution fusion | flops 1610612736 | bytes 6815744 | tf_op jit(solution)/shard_map/dot_general | solution.py:18
  64.4 19.1 %attend.1 = (bf16[1024,768]{1,0:T(8,128)(2,1)S(1)}, bf16[1024,256]{1,0:T(8,128)(2,1)S(1)}, f32[2,2,1024]{2,1,0:T(2,128)S(1)}) custom-call(s32[2,4]{1,0:T(2,128)S(1)} %pad_add_fusion.reach_ref, f32[1024,768]{1,0:T(8,128)} %fusion.25.mixed_ref, f32[1024,64]{1,0:T(8,128)S(1)} %get-tuple-element.72.cos_ref, f32[1024,64]{1,0:T(8,128)S(1)} %get-tuple-element.73.sin_ref, ...), custom_call_target="tpu_custom_call" | custom-call | flops 1073741824 | bytes 6291456 | tf_op jit(solution)/shard_map/attend/pallas_call | solution.py:167
  83.5 0.7 convolution_convert_fusion.2.refs_0_
  84.3 0.0 copy-start.25
  84.3 16.1 %reduce_sums.3 = f32[256,1024]{1,0:T(8,128)S(1)} custom-call(bf16[1024,1024]{1,0:T(8,128)(2,1)S(1)} %convolution_convert_fusion.2.refs_0_), custom_call_target="tpu_custom_call" | custom-call | tf_op jit(solution)/shard_map/reduce_sums/pallas_call | solution.py:494
  100.4 0.2 fusion.24
  100.6 0.2 multiply_reduce_fusion.2
  100.9 0.7 copy-done.23
  101.6 0.2 multiply_convert_fusion.2.refs_0_
  101.8 37.0 %gather_parts.4 = (bf16[1024,1024]{1,0:T(8,128)(2,1)S(1)}, bf16[656,1024]{1,0:T(8,128)(2,1)S(1)}) custom-call(bf16[256,1024]{1,0:T(8,128)(2,1)S(1)} %multiply_convert_fusion.2.refs_0_, bf16[656,128]{1,0:T(8,128)(2,1)S(1)} %copy-done.7), custom_call_target="tpu_custom_call" | custom-call | tf_op jit(solution)/shard_map/gather_parts/pallas_call | solution.py:494
  138.8 1.3 copy-done.14
  140.2 6.0 %fusion.26 = f32[1024,1312]{0,1:T(8,128)S(1)} fusion(bf16[1024,1024]{1,0:T(8,128)(2,1)} %copy-done.14, bf16[1024,1312]{0,1:T(8,128)(2,1)} %all-gather.2.cloned.1.call-done), kind=kOutput, calls=%fused_computation.80 | convolution fusion | flops 2751463424 | bytes 10158080 | tf_op jit(solution)/shard_map/dot_general | solution.py:18
  146.1 3.0 fusion.4
  149.2 1.6 convolution_convert_fusion.6.refs_1_
  150.8 0.4 copy-done.34
  151.2 1.0 copy-done.15
  152.2 5.4 %convolution_convert_fusion = bf16[1024,1312]{0,1:T(8,128)(2,1)} fusion(bf16[1024,1024]{1,0:T(8,128)(2,1)S(1)} %copy-done.15, bf16[1024,656]{0,1:T(8,128)(2,1)S(1)} %get-tuple-element.63, bf16[1024,656]{0,1:T(8,128)(2,1)S(1)} %get-tuple-element.62), kind=kOutput, calls=%fused_computation.1 | convolution fusion | flops 2758180864 | bytes 7471104 | tf_op jit(solution)/shard_map/dot_general | solution.py:22
  157.6 4.5 %copy.36 = bf16[1024,1312]{1,0:T(8,128)(2,1)} copy(bf16[1024,1312]{0,1:T(8,128)(2,1)} %convolution_convert_fusion) | data formatting | bytes 5373952
  162.1 0.0 reduce-scatter.4.cloned.1.call-update
  162.2 6.1 %convolution_convert_fusion.1.refs_0_ = bf16[1024,1024]{1,0:T(8,128)(2,1)S(1)} fusion(bf16[1024,1312]{0,1:T(8,128)(2,1)} %all-gather.2.cloned.1.call-done, bf16[1024,656]{0,1:T(8,128)(2,1)} %copy-done.34, bf16[1024,656]{0,1:T(8,128)(2,1)} %copy-done.33), kind=kOutput, calls=%fused_computation.12 | convolution fusion | flops 2757885952 | bytes 7471104 | tf_op jit(solution)/shard_map/dot_general | solution.py:28
  168.2 36.4 %reduce_sums.4 = (f32[256,1024]{1,0:T(8,128)S(1)}, f32[656,128]{1,0:T(8,128)S(1)}) custom-call(bf16[1024,1024]{1,0:T(8,128)(2,1)S(1)} %convolution_convert_fusion.1.refs_0_, bf16[656,1024]{1,0:T(8,128)(2,1)S(1)} %convolution_convert_fusion.6.refs_1_), custom_call_target="tpu_custom_call" | custom-call | tf_op jit(solution)/shard_map/reduce_sums/pallas_call | solution.py:494
  204.7 0.5 multiply_reduce_fusion
  205.2 1.4 fusion.23
  206.6 15.3 %gather_parts.5 = bf16[1024,1024]{1,0:T(8,128)(2,1)S(1)} custom-call(bf16[256,1024]{1,0:T(8,128)(2,1)S(1)} %get-tuple-element.58.refs_0_), custom_call_target="tpu_custom_call" | custom-call | tf_op jit(solution)/shard_map/gather_parts/pallas_call | solution.py:494
  221.9 0.7 convolution_convert_fusion.8.ga_ref
  222.7 0.3 copy-done.2
  223.0 0.5 copy-done.22
  223.5 18.5 %attend_back.1 = bf16[1024,768]{1,0:T(8,128)(2,1)S(1)} custom-call(s32[2,4]{1,0:T(2,128)S(1)} %pad_add_fusion.reach_ref, bf16[1024,768]{1,0:T(8,128)(2,1)S(1)} %copy-done.22, bf16[1024,256]{1,0:T(8,128)(2,1)S(1)} %convolution_convert_fusion.8.ga_ref, bf16[1024,256]{1,0:T(8,128)(2,1)S(1)} %get-tuple-element.28.att_ref, ...), custom_call_target="tpu_custom_call" | custom-call | flops 2684354560 | bytes 6291456 | tf_op jit(solution)/shard_map/attend_back/pallas_call | solution.py:203
  242.1 0.7 convolution_convert_fusion.7.refs_3_
  242.8 0.6 copy-done.20
  243.4 0.4 copy-done.32
  243.8 1.9 convolution_convert_fusion.3.refs_1_
  245.7 1.8 convolution_convert_fusion.4.refs_0_
  247.5 1.9 convolution_convert_fusion.5.refs_2_
  249.4 48.8 %reduce_sums.5 = (f32[256,1024]{1,0:T(8,128)S(1)}, f32[256,1024]{1,0:T(8,128)S(1)}, f32[128,768]{1,0:T(8,128)S(1)}, f32[256,128]{1,0:T(8,128)S(1)}) custom-call(bf16[1024,1024]{1,0:T(8,128)(2,1)S(1)} %convolution_convert_fusion.4.refs_0_, bf16[1024,1024]{1,0:T(8,128)(2,1)S(1)} %convolution_convert_fusion.3.refs_1_, ...), custom_call_target="tpu_custom_call" | custom-call | tf_op jit(solution)/shard_map/reduce_sums/pallas_call | solution.py:494
  298.2 0.6 fusion.17
  298.8 9.3 %sum_gains.1 = f32[8,256]{1,0:T(8,128)S(1)} custom-call(f32[8,256]{1,0:T(8,128)S(1)} %reshape.119.part_ref), custom_call_target="tpu_custom_call" | custom-call | tf_op jit(solution)/shard_map/sum_gains/pallas_call | solution.py:494
  308.2 0.6 copy.39
  308.8 0.6 copy.38
  309.4 0.9 copy.35
  310.3 2.3 add_convert_fusion
  312.6 1.2 fusion.16
  313.8 1.2 copy.37
  315.0 0.9 convert.9
  315.9 0.7 copy.42
  316.6 0.7 copy.43
  (76 shorter events, 0.2 us)
Async XLA Ops:
  7.2 5.1 %copy-start = (bf16[256,1024]{1,0:T(8,128)(2,1)S(1)}, bf16[256,1024]{1,0:T(8,128)(2,1)}, u32[]{:S(2)}) copy-start(bf16[256,1024]{1,0:T(8,128)(2,1)} %refs_1_.2) | copy-start | bytes 1572868
  7.2 5.1 %copy-start.8 = (bf16[256,128]{1,0:T(8,128)(2,1)S(1)}, bf16[256,128]{1,0:T(8,128)(2,1)}, u32[]{:S(2)}) copy-start(bf16[256,128]{1,0:T(8,128)(2,1)} %refs_3_.1) | copy-start | bytes 196612
  7.2 50.7 %copy-start.30 = (s32[1,3]{1,0:T(1,128)S(1)}, s32[1,3]{1,0:T(1,128)}, u32[]{:S(2)}) copy-start(s32[1,3]{1,0:T(1,128)} %param.16) | copy-start | bytes 40
  7.2 133.0 %all-gather.2.cloned.1.call-start = ((), (), s32[]{:S(2)}) async-start(), calls=%async_computation.1 | async-start | bytes 3022848 | tf_op jit(solution)/shard_map/all_gather | solution.py:901
  54.0 1.4 copy-start.9
  55.4 1.3 copy-start.12
  56.7 1.1 copy-start.16
  57.8 25.7 %copy-start.3 = (bf16[256,1024]{1,0:T(8,128)(2,1)}, bf16[256,1024]{1,0:T(8,128)(2,1)S(1)}, u32[]{:S(2)}) copy-start(bf16[256,1024]{1,0:T(8,128)(2,1)S(1)} %get-tuple-element.29) | copy-start | bytes 1572868
  57.9 255.9 %reduce-scatter.4.cloned.1.call-start = ((), (), s32[]{:S(2)}) async-start(), calls=%async_computation.2 | async-start | bytes 3244032
  58.5 5.9 %copy-start.1 = (s32[1024,1]{1,0:T(8,128)}, s32[1024,1]{1,0:T(8,128)S(1)}, u32[]{:S(2)}) copy-start(s32[1024,1]{1,0:T(8,128)S(1)} %copy.33.segc_ref) | copy-start | bytes 12292
  58.7 2.3 copy-start.10
  58.7 2.3 copy-start.17
  83.5 16.9 %copy-start.21 = (bf16[1024,768]{1,0:T(8,128)(2,1)}, bf16[1024,768]{1,0:T(8,128)(2,1)S(1)}, u32[]{:S(2)}) copy-start(bf16[1024,768]{1,0:T(8,128)(2,1)S(1)} %get-tuple-element.30.qkv_ref) | copy-start | bytes 4718596
  84.3 16.1 %copy-start.25 = (bf16[256,1024]{1,0:T(8,128)(2,1)S(1)}, bf16[256,1024]{1,0:T(8,128)(2,1)}, u32[]{:S(2)}) copy-start(bf16[256,1024]{1,0:T(8,128)(2,1)} %param.9) | copy-start | bytes 1572868
  100.4 1.2 copy-start.29
  100.4 1.4 copy-start.7
  100.6 1.0 copy-start.23
  138.8 1.3 copy-start.14
  140.2 6.0 %copy-start.19 = (bf16[656,1024]{1,0:T(8,128)(2,1)}, bf16[656,1024]{1,0:T(8,128)(2,1)S(1)}, u32[]{:S(2)}) copy-start(bf16[656,1024]{1,0:T(8,128)(2,1)S(1)} %get-tuple-element.32) | copy-start | bytes 4030468
  140.2 6.0 %copy-start.13 = (bf16[1024,1024]{1,0:T(8,128)(2,1)S(1)}, bf16[1024,1024]{1,0:T(8,128)(2,1)}, u32[]{:S(2)}) copy-start(bf16[1024,1024]{1,0:T(8,128)(2,1)} %copy-done.12) | copy-start | bytes 6291460
  149.2 1.6 copy-start.31
  149.2 1.6 copy-start.33
  149.2 2.0 copy-start.34
  149.2 3.0 copy-start.15
  168.2 36.4 %copy-start.24 = (f32[256,1024]{1,0:T(8,128)S(1)}, f32[256,1024]{1,0:T(8,128)}, u32[]{:S(2)}) copy-start(f32[256,1024]{1,0:T(8,128)} %copy-done.23) | copy-start | bytes 3145732
  204.6 2.0 copy-start.5
  206.6 15.3 %copy-start.4 = (bf16[256,1024]{1,0:T(8,128)(2,1)S(1)}, bf16[256,1024]{1,0:T(8,128)(2,1)}, u32[]{:S(2)}) copy-start(bf16[256,1024]{1,0:T(8,128)(2,1)} %copy-done.3) | copy-start | bytes 1572868
  221.9 1.0 copy-start.2
  221.9 1.6 copy-start.22
  242.0 1.3 copy-start.20
  242.1 1.7 copy-start.32
  243.8 1.9 copy-start.18
  245.7 1.8 copy-start.11
  249.4 48.8 %copy-start.26 = (bf16[256,1024]{1,0:T(8,128)(2,1)S(1)}, bf16[256,1024]{1,0:T(8,128)(2,1)}, u32[]{:S(2)}) copy-start(bf16[256,1024]{1,0:T(8,128)(2,1)} %param.9) | copy-start | bytes 1572868
  249.4 48.8 %copy-start.28 = (f32[1024]{0:T(1024)S(1)}, f32[1024]{0:T(1024)}, u32[]{:S(2)}) copy-start(f32[1024]{0:T(1024)} %param.10) | copy-start | bytes 12292
  310.3 2.3 copy-start.27
  312.6 4.0 %copy-start.6 = (f32[656,128]{1,0:T(8,128)S(1)}, f32[656,128]{1,0:T(8,128)}, u32[]{:S(2)}) copy-start(f32[656,128]{1,0:T(8,128)} %copy-done.5) | copy-start | bytes 1007620
Sparse Core Ops, SparseCore 0:
  58.0 67.4 all-gather.1
  162.3 84.4 reduce-scatter.3
